TPU v7x, 32 devices: a whole 2x2x4 slice. The times are simulated.
32 devices in a mesh: dp: 4 (over z), ctx: 4 (over x, core), tensor: 2 (over y).
Axes of the slice: x: 2, y: 2, z: 4, core: 2. Of those that a mesh axis runs over, the one named last changes fastest.
Arguments:
- layer_input: bfloat16 [4, 1024, 2048], P('dp', 'ctx'), may hold values from -6 to 6
- output_grad: bfloat16 [4, 1024, 2048], P('dp', 'ctx'), may hold values from -6 to 6
- prefix: int32 [4], P('dp'), may hold values from 204 to 1024
- attn_gain: float32 [2048], replicated, may hold values from 0.1 to 1.9
- w_query: bfloat16 [2048, 2048], P(None, 'tensor'), may hold values from -0.125 to 0.125
- w_key: bfloat16 [2048, 512], P(None, 'tensor'), may hold values from -0.125 to 0.125
- w_value: bfloat16 [2048, 512], P(None, 'tensor'), may hold values from -0.125 to 0.125
- w_out: bfloat16 [2048, 2048], P('tensor'), may hold values from -1 to 1
- mlp_gain: float32 [2048], replicated, may hold values from 0.1 to 1.9
- w_gate: bfloat16 [2048, 8192], P(None, 'tensor'), may hold values from -0.125 to 0.125
- w_up: bfloat16 [2048, 8192], P(None, 'tensor'), may hold values from -0.125 to 0.125
- w_down: bfloat16 [8192, 2048], P('tensor'), may hold values from -0.0625 to 0.0625
Outputs:
- layer_output: bfloat16 [4, 1024, 2048], P('dp', 'ctx')
- input_grad: float32 [4, 1024, 2048], P('dp', 'ctx')
- d_attn_gain: float32 [2048], P(('dp', 'ctx'))
- d_query: float32 [2048, 2048], P(('dp', 'ctx'), 'tensor')
- d_key: float32 [2048, 512], P(('dp', 'ctx'), 'tensor')
- d_value: float32 [2048, 512], P(('dp', 'ctx'), 'tensor')
- d_out_proj: float32 [2048, 2048], P('tensor', ('dp', 'ctx'))
- d_mlp_gain: float32 [2048], P(('dp', 'ctx'))
- d_gate: float32 [2048, 8192], P(('dp', 'ctx'), 'tensor')
- d_up: float32 [2048, 8192], P(('dp', 'ctx'), 'tensor')
- d_down: float32 [8192, 2048], P('tensor', ('dp', 'ctx'))
All inputs are finite; a program needn't handle non-finite values.
Results may differ from a plain program's by a relative error of at most 0.024.
Values may be sent and summed in bfloat16 or wider, within the bound.
A program may use at most 256 MiB of HBM per device.

v0:
```python
import functools
import jax
import jax.numpy as jnp
from jax import lax
from jax.experimental import pallas as pl
from jax.experimental.pallas import tpu as pltpu
from jax.sharding import PartitionSpec as P

HD = 64
EPS = 1e-05
ROPE_BASE = 500000.0
NEG = -1e30
BF = jnp.bfloat16
F32 = jnp.float32
VMEM_MOST = 60 * 1024 * 1024


def cost(flops, nbytes, trans=0):
    return pl.CostEstimate(flops=int(flops), bytes_accessed=int(nbytes), transcendentals=int(trans))


def nt(a, b):
    return lax.dot_general(a, b, (((1,), (1,)), ((), ())), preferred_element_type=F32)


def tn(a, b):
    return lax.dot_general(a, b, (((0,), (0,)), ((), ())), preferred_element_type=F32)


def nn(a, b):
    return jnp.dot(a, b, preferred_element_type=F32)


def swap_halves(t):
    lane = lax.broadcasted_iota(jnp.int32, t.shape, 1) % HD
    n = t.shape[1]
    return jnp.where(
        lane < HD // 2, pltpu.roll(t, n - HD // 2, 1), pltpu.roll(t, HD // 2, 1)
    )


def rope_tables(first, span):
    position = (first + jnp.arange(span)).astype(F32)
    frequency = ROPE_BASE ** (-jnp.arange(HD // 2).astype(F32) * 2.0 / HD)
    angle = position[:, None] * frequency[None, :]
    cosine, sine = jnp.cos(angle), jnp.sin(angle)
    return (
        jnp.concatenate([cosine, cosine, cosine, cosine], axis=1),
        jnp.concatenate([-sine, sine, -sine, sine], axis=1),
    )


def mask_bias(first, prefix, length, span):
    key = lax.broadcasted_iota(jnp.int32, (length, span), 0)
    query = lax.broadcasted_iota(jnp.int32, (length, span), 1) + first
    return jnp.where((key <= query) | (key < prefix), 0.0, NEG).astype(F32)


def gate_parts(gate, up, d_act):
    sig = 1.0 / (1.0 + jnp.exp(-gate))
    silu = gate * sig
    return (
        (silu * up).astype(BF),
        (d_act * up * (sig + silu * (1.0 - sig))).astype(BF),
        (d_act * silu).astype(BF),
    )


MESH = pl.DeviceIdType.MESH


def remote(src, dst, send, recv, to):
    return pltpu.make_async_remote_copy(
        src_ref=src, dst_ref=dst, send_sem=send, recv_sem=recv, device_id=to, device_id_type=MESH
    )


def enter(devices):
    barrier = pltpu.get_barrier_semaphore()
    for to in devices:
        pl.semaphore_signal(barrier, inc=1, device_id=to, device_id_type=MESH)
    pl.semaphore_wait(barrier, len(devices))


def around(z, ndp):
    return [{"dp": lax.rem(z + 1, ndp)}, {"dp": lax.rem(z + ndp - 1, ndp)}]


def mates(me, y):
    return [{"ctx": me ^ 1}, {"ctx": me ^ 2}, {"ctx": me ^ 3}, {"tensor": 1 - y}]


class Relay:
    def __init__(self, z, ndp, hop, own, blocks, sems):
        self.z, self.ndp, self.hop = z, ndp, hop
        self.own, self.blocks, self.sems = own, blocks, sems

    def copy(self, way, block, to):
        src = self.own if self.hop == 1 else self.blocks.at[block]
        at = 0 if way > 0 else 1
        return remote(
            src, self.blocks.at[block], self.sems.at[0, at], self.sems.at[1, at], {"dp": to}
        )

    def each(self, act, incoming):
        z, hop = self.z, self.hop
        for way in (1, -1):
            if incoming:
                block = z - way * hop
                ok = block >= 0 if way > 0 else block < self.ndp
            else:
                block = z - way * (hop - 1)
                ok = (block >= 0) & (z < self.ndp - 1) if way > 0 else (block < self.ndp) & (z > 0)

            @pl.when(ok)
            def _(way=way, block=block):
                act(self.copy(way, block, z if incoming else z + way))

    def start(self):
        self.each(lambda c: c.start(), False)

    def wait_recv(self):
        self.each(lambda c: c.wait_recv(), True)

    def wait_send(self):
        self.each(lambda c: c.wait_send(), False)


def rope_parts(t, cosine, sine):
    pieces = []
    for i in range(t.shape[1] // 128):
        part = t[:, 128 * i : 128 * (i + 1)]
        pieces.append((part * cosine + swap_halves(part) * sine).astype(BF))
    return pieces


def front_kernel(
    ndp, nctx, group,
    where_ref, x_ref, gain1_ref, wq_hbm, wk_hbm, wv_hbm, wo_hbm, cos_ref, sin_ref, gain2_ref, og_hbm,
    n1_ref, q_ref, kv_out, att_ref, lse_ref, resid_ref, n2_ref, og_all,
    n1_buf, wq, wk, wv, wo, kv, bias_ref, part, part_got,
    w_sem, kv_sem, kv_out_sem, part_sem, z_sem,
):
    z, me, y = lax.axis_index("dp"), lax.axis_index("ctx"), lax.axis_index("tensor")
    span, width = x_ref.shape
    length = kv.shape[0]
    kvw = wk.shape[1]
    loads = [
        pltpu.make_async_copy(src, dst, w_sem.at[i])
        for i, (src, dst) in enumerate(((wk_hbm, wk), (wv_hbm, wv), (wq_hbm, wq), (wo_hbm, wo)))
    ]
    for copy in loads:
        copy.start()
    hop1 = Relay(z, ndp, 1, og_hbm, og_all, z_sem.at[0])
    hop2 = Relay(z, ndp, 2, og_hbm, og_all, z_sem.at[1])
    enter(around(z, ndp) + mates(me, y))
    hop1.start()
    v = x_ref[...].astype(F32)
    factor = lax.rsqrt(jnp.mean(v * v, axis=-1, keepdims=True) + EPS)
    n1_buf[...] = (v * factor * gain1_ref[...]).astype(BF)
    cosine, sine = cos_ref[...], sin_ref[...]
    mine = pl.ds(pl.multiple_of(me * span, span), span)
    loads[0].wait()
    for i, piece in enumerate(rope_parts(nn(n1_buf[...], wk[...]), cosine, sine)):
        kv[mine, 128 * i : 128 * (i + 1)] = piece
    loads[1].wait()
    kv[mine, kvw:] = nn(n1_buf[...], wv[...]).astype(BF)

    def kv_copy(which, block, mask):
        rows = pl.ds(pl.multiple_of(block * span, span), span)
        return remote(kv.at[rows], kv.at[rows], kv_sem.at[0, which], kv_sem.at[1, which], {"ctx": me ^ mask})

    to_x = kv_copy(0, me, 2)
    to_core = kv_copy(1, me, 1)
    onward = kv_copy(2, me ^ 2, 1)
    to_x.start()
    to_core.start()
    loads[2].wait()
    for i, piece in enumerate(rope_parts(nn(n1_buf[...], wq[...]), cosine, sine)):
        q_ref[:, 128 * i : 128 * (i + 1)] = piece
    part_width = width // (ndp * nctx)
    for p in range(nctx):
        for b in range(ndp):
            at = (b * nctx + p) * part_width
            n1_ref[p, :, b * part_width : (b + 1) * part_width] = n1_buf[:, at : at + part_width]
    bias_ref[...] = mask_bias(where_ref[0], where_ref[1], length, span)
    to_x.wait_recv()
    onward.start()
    to_core.wait_recv()
    onward.wait_recv()
    to_x.wait_send()
    to_core.wait_send()
    onward.wait_send()
    save_kv = pltpu.make_async_copy(kv, kv_out, kv_out_sem)
    save_kv.start()

    wide = 128 * group
    heads = wide // HD

    @pl.loop(0, kvw // 128)
    def _(j):
        lanes = pl.ds(pl.multiple_of(j * wide, 128), wide)
        queries = q_ref[:, lanes] * jnp.asarray(HD**-0.5, BF)
        keys = kv[:, pl.ds(pl.multiple_of(j * 128, 128), 128)]
        values = kv[:, pl.ds(pl.multiple_of(kvw + j * 128, 128), 128)]
        rows, outs = [], []
        for h in range(heads):
            at = slice(HD * (h // group), HD * (h // group + 1))
            scores = nt(keys[:, at], queries[:, HD * h : HD * (h + 1)]) + bias_ref[...]
            top = jnp.max(scores, axis=0, keepdims=True)
            exponent = jnp.exp(scores - top)
            total = jnp.sum(exponent, axis=0, keepdims=True)
            rows.append(top + jnp.log(total))
            outs.append(tn(values[:, at], exponent.astype(BF)) / total)
            if h % 2:
                both = jnp.concatenate(outs, axis=0).T.astype(BF)
                att_ref[:, pl.ds(pl.multiple_of(j * wide + HD * (h - 1), 128), 128)] = both
                outs = []
        lse_ref[pl.ds(pl.multiple_of(j * heads, heads), heads), :] = jnp.concatenate(rows, axis=0)

    hop1.wait_recv()
    hop2.start()
    save_kv.wait()
    loads[3].wait()
    count, _, cols = part.shape
    copies = [
        remote(part.at[c], part_got.at[c], part_sem.at[0, c], part_sem.at[1, c], {"tensor": 1 - y})
        for c in range(count)
    ]
    for c in range(count):
        part[c] = nn(att_ref[...], wo[:, c * cols : (c + 1) * cols]).astype(BF)
        copies[c].start()
    square = jnp.zeros((span, 1), F32)
    for c in range(count):
        at = slice(c * cols, (c + 1) * cols)
        copies[c].wait_recv()
        r = x_ref[:, at].astype(F32) + (part[c].astype(F32) + part_got[c].astype(F32))
        resid_ref[:, at] = r
        square += jnp.sum(r * r, axis=-1, keepdims=True)
    factor = lax.rsqrt(square / width + EPS)
    for c in range(count):
        at = slice(c * cols, (c + 1) * cols)
        n2_ref[:, at] = (resid_ref[:, at] * factor * gain2_ref[:, at]).astype(BF)
    for copy in copies:
        copy.wait_send()
    hop1.wait_send()
    hop2.wait_recv()
    hop2.wait_send()


HBM_SPEC = pl.BlockSpec(memory_space=pl.ANY)
VMEM_SPEC = pl.BlockSpec(memory_space=pltpu.VMEM)
SMEM_SPEC = pl.BlockSpec(memory_space=pltpu.SMEM)


def own(number):
    return pltpu.CompilerParams(
        vmem_limit_bytes=VMEM_MOST, collective_id=number, has_side_effects=True
    )


def front(where, x, gain1, wq, wk, wv, wo, cosine, sine, gain2, og, ndp, nctx):
    span, width = x.shape
    qw, kvw = wq.shape[1], wk.shape[1]
    group = qw // kvw
    length = span * nctx
    chunks = 4
    dma = pltpu.SemaphoreType.DMA
    return pl.pallas_call(
        functools.partial(front_kernel, ndp, nctx, group),
        in_specs=[SMEM_SPEC, VMEM_SPEC, VMEM_SPEC] + [HBM_SPEC] * 4 + [VMEM_SPEC] * 3 + [HBM_SPEC],
        out_specs=[VMEM_SPEC, VMEM_SPEC, HBM_SPEC] + [VMEM_SPEC] * 4 + [HBM_SPEC],
        out_shape=[
            jax.ShapeDtypeStruct((nctx, span, width // nctx), BF),
            jax.ShapeDtypeStruct((span, qw), BF),
            jax.ShapeDtypeStruct((length, 2 * kvw), BF),
            jax.ShapeDtypeStruct((span, qw), BF),
            jax.ShapeDtypeStruct((qw // HD, span), F32),
            jax.ShapeDtypeStruct((span, width), F32),
            jax.ShapeDtypeStruct((span, width), BF),
            jax.ShapeDtypeStruct((ndp, span, width), BF),
        ],
        scratch_shapes=[
            pltpu.VMEM((span, width), BF),
            pltpu.VMEM((width, qw), BF),
            pltpu.VMEM((width, kvw), BF),
            pltpu.VMEM((width, kvw), BF),
            pltpu.VMEM((qw, width), BF),
            pltpu.VMEM((length, 2 * kvw), BF),
            pltpu.VMEM((length, span), F32),
            pltpu.VMEM((chunks, span, width // chunks), BF),
            pltpu.VMEM((chunks, span, width // chunks), BF),
            dma((4,)),
            dma((2, 3)),
            dma,
            dma((2, chunks)),
            dma((2, 2, 2)),
        ],
        compiler_params=own(0),
        cost_estimate=cost(2 * span * width * (2 * qw + 2 * kvw), 4 * width * (qw + kvw)),
        name="front",
    )(where, x, gain1.reshape(1, width), wq, wk, wv, wo, cosine, sine, gain2.reshape(1, width), og)


def halves(y, span):
    return pl.ds(pl.multiple_of(y * (span // 2), span // 2), span // 2)


class Far:
    def __init__(self, z, y, blocks, far, sems):
        self.z, self.far = z, far
        rows = halves(y, far.shape[0])
        block = jnp.where(z == 1, 3, 0)
        to = jnp.where(z == 1, 0, 3)
        self.over = remote(
            blocks.at[block, rows], far.at[rows], sems.at[0, 0], sems.at[1, 0], {"dp": to}
        )
        self.swap = remote(
            far.at[rows], far.at[rows], sems.at[0, 1], sems.at[1, 1], {"tensor": 1 - y}
        )
        self.gives = (z == 1) | (z == 2)
        self.takes = (z == 0) | (z == 3)

    def start(self):
        pl.when(self.gives)(lambda: self.over.start())

    def onward(self):
        @pl.when(self.takes)
        def _():
            self.over.wait_recv()
            self.swap.start()

    def wait_recv(self):
        pl.when(self.takes)(lambda: self.swap.wait_recv())

    def finish(self):
        pl.when(self.takes)(lambda: self.swap.wait_send())
        pl.when(self.gives)(lambda: self.over.wait_send())


class Gather:
    def __init__(self, z, y, ndp, own, blocks, sems, swaps):
        self.z, self.y, self.ndp = z, y, ndp
        self.own, self.blocks, self.sems, self.swaps = own, blocks, sems, swaps
        self.rows = halves(y, own.shape[0])

    def over(self, way, hop, block, to):
        src = self.own.at[self.rows] if hop == 1 else self.blocks.at[block, self.rows]
        at = 0 if way > 0 else 1
        return remote(
            src, self.blocks.at[block, self.rows],
            self.sems.at[hop - 1, 0, at], self.sems.at[hop - 1, 1, at], {"dp": to},
        )

    def swap(self, way, hop, block):
        at = 0 if way > 0 else 1
        part = self.blocks.at[block, self.rows]
        return remote(
            part, part, self.swaps.at[hop - 1, 0, at], self.swaps.at[hop - 1, 1, at],
            {"tensor": 1 - self.y},
        )

    def comes(self, way, hop):
        block = self.z - way * hop
        return block, (block >= 0 if way > 0 else block < self.ndp)

    def leaves(self, way, hop):
        block = self.z - way * (hop - 1)
        if way > 0:
            return block, (block >= 0) & (self.z < self.ndp - 1)
        return block, (block < self.ndp) & (self.z > 0)

    def send(self, hop):
        for way in (1, -1):
            block, ok = self.leaves(way, hop)

            @pl.when(ok)
            def _(way=way, block=block):
                self.over(way, hop, block, self.z + way).start()

    def step(self, hop):
        for way in (1, -1):
            block, ok = self.comes(way, hop)

            @pl.when(ok)
            def _(way=way, block=block):
                self.over(way, hop, block, self.z).wait_recv()
                self.swap(way, hop, block).start()

        if hop < self.ndp - 1:
            self.send(hop + 1)

    def finish(self):
        for hop in range(1, self.ndp):
            for way in (1, -1):
                block, ok = self.comes(way, hop)

                @pl.when(ok)
                def _(way=way, block=block, hop=hop):
                    self.swap(way, hop, block).wait()

                block, ok = self.leaves(way, hop)

                @pl.when(ok)
                def _(way=way, block=block, hop=hop):
                    self.over(way, hop, block, self.z + way).wait_send()


def middle_kernel(
    ndp, nctx,
    n_ref, g_ref, wg_ref, wu_ref, wd_ref, n_hbm, n1_hbm, att_hbm, g_near,
    o_ref, dn_ref, n_all, n1_all, att_all, g_far,
    o_acc, dn_acc,
    z_sem, swap_sem, n1_sem, att_sem, far_sem,
):
    z, me, y = lax.axis_index("dp"), lax.axis_index("ctx"), lax.axis_index("tensor")
    j = pl.program_id(0)
    last = pl.num_programs(0) - 1
    gather = Gather(z, y, ndp, n_hbm, n_all, z_sem, swap_sem)
    far = Far(z, y, g_near, g_far, far_sem)
    spreads = []
    for m in range(1, nctx):
        spreads.append(
            remote(n1_hbm.at[me ^ m], n1_all.at[me], n1_sem.at[0, m], n1_sem.at[1, m], {"ctx": me ^ m})
        )
        spreads.append(
            remote(att_hbm, att_all.at[me], att_sem.at[0, m], att_sem.at[1, m], {"ctx": me ^ m})
        )

    @pl.when(j == 0)
    def _():
        enter(around(z, ndp) + mates(me, y))
        gather.send(1)
        far.start()
        for copy in spreads:
            copy.start()

    normed2, grad = n_ref[...], g_ref[...]
    gate = nn(normed2, wg_ref[...])
    up = nn(normed2, wu_ref[...])
    d_act = nt(grad, wd_ref[...])
    act, d_gate, d_up = gate_parts(gate, up, d_act)

    @pl.when(j == 0)
    def _():
        o_acc[...] = nn(act, wd_ref[...])
        dn_acc[...] = nt(d_gate, wg_ref[...]) + nt(d_up, wu_ref[...])

    @pl.when(j > 0)
    def _():
        o_acc[...] += nn(act, wd_ref[...])
        dn_acc[...] += nt(d_gate, wg_ref[...]) + nt(d_up, wu_ref[...])

    @pl.when(j == 3)
    def _():
        gather.step(1)

    @pl.when(j == 5)
    def _():
        gather.step(2)
        far.onward()

    @pl.when(j == last)
    def _():
        gather.step(3)
        o_ref[...] = o_acc[...].astype(BF)
        dn_ref[...] = dn_acc[...].astype(BF)
        for copy in spreads:
            copy.wait()
        far.wait_recv()
        far.finish()
        gather.finish()


def middle(n2, og, wg, wu, wd, n1p, att, og_all, ndp, nctx, step=512):
    span, width = n2.shape
    units = wg.shape[1]
    dma = pltpu.SemaphoreType.DMA
    whole = pl.BlockSpec((span, width), lambda j: (0, 0))
    cols = pl.BlockSpec((width, step), lambda j: (0, j))
    return pl.pallas_call(
        functools.partial(middle_kernel, ndp, nctx),
        grid=(units // step,),
        in_specs=[
            whole, whole, cols, cols, pl.BlockSpec((step, width), lambda j: (j, 0)),
            HBM_SPEC, HBM_SPEC, HBM_SPEC, HBM_SPEC,
        ],
        out_specs=[whole, whole, HBM_SPEC, HBM_SPEC, HBM_SPEC, HBM_SPEC],
        out_shape=[
            jax.ShapeDtypeStruct((span, width), BF),
            jax.ShapeDtypeStruct((span, width), BF),
            jax.ShapeDtypeStruct((ndp, span, width), BF),
            jax.ShapeDtypeStruct((nctx, span, width // nctx), BF),
            jax.ShapeDtypeStruct((nctx,) + att.shape, BF),
            jax.ShapeDtypeStruct((span, width), BF),
        ],
        scratch_shapes=[
            pltpu.VMEM((span, width), F32),
            pltpu.VMEM((span, width), F32),
            dma((ndp - 1, 2, 2)),
            dma((ndp - 1, 2, 2)),
            dma((2, nctx)),
            dma((2, nctx)),
            dma((2, 2)),
        ],
        compiler_params=own(1),
        cost_estimate=cost(12 * span * width * units, 6 * width * units),
        name="middle",
    )(n2, og, wg, wu, wd, n2, n1p, att, og_all)


def rear_kernel(
    ndp, nctx, group, chunk, rows,
    where_ref, q_ref, kv_ref, lse_ref, cos_ref, sin_ref, gain_ref, dn_ref,
    n_own, n_near, g_own, g_near, g_far, wg_hbm, wu_hbm, wd_hbm, wq_hbm, wk_hbm, wv_hbm, wo_hbm,
    resid_hbm, n1_own, n1_near, att_own, att_near, out_hbm,
    down_z, gate_z, up_z, att_z, front_out, front_got, out_got, dr_out, gain_grad_ref,
    n_all, g_all, acts, wg_buf, wu_buf, wd_buf, give, take, x_give, x_take, x_keep,
    left1, left2, right1, right2, prod, low, d_att, bias_ref, dkv, land, acc,
    in_sem, l_sem, w_sem, back_sem, dn_sem, low_sem, dkv_sem, r_sem, core_sem, x_sem, zz_sem, z_own,
    att_sem, y_sem, save_sem,
):
    z, me, y = lax.axis_index("dp"), lax.axis_index("ctx"), lax.axis_index("tensor")
    tokens, width = n_all.shape
    span, qw = q_ref.shape
    length = kv_ref.shape[0]
    kvw = kv_ref.shape[1] // 2
    units = acts.shape[1]
    core, xpos = me % 2, me // 2
    part = width // (ndp * nctx)
    start = z * units
    peers = [{"dp": lax.rem(z + s, ndp)} for s in range(1, ndp)]
    mate = {"tensor": 1 - y}
    mine = pl.ds(pl.multiple_of(me * span, span), span)
    cross = pl.ds(pl.multiple_of((me ^ 2) * span, span), span)

    def block_load(r, own_ref, near, far, dst, sem):
        block = lax.rem(jnp.where(z < ndp // 2, z + r, z + ndp - r), ndp)
        at = dst.at[pl.ds(r * span, span)]
        if r == 0:
            return [(None, pltpu.make_async_copy(own_ref, at, sem))]
        if r < ndp - 1 or far is None:
            return [(None, pltpu.make_async_copy(near.at[block], at, sem))]
        end = (z == 0) | (z == ndp - 1)
        return [
            (end, pltpu.make_async_copy(far, at, sem)),
            (jnp.logical_not(end), pltpu.make_async_copy(near.at[block], at, sem)),
        ]

    def go(copies):
        for ok, copy in copies:
            if ok is None:
                copy.start()
            else:
                pl.when(ok)(lambda copy=copy: copy.start())

    def done(copies):
        copies[0][1].wait()

    n_loads = [block_load(r, n_own, n_near, None, n_all, in_sem.at[0, r]) for r in range(ndp)]
    g_loads = [block_load(r, g_own, g_near, g_far, g_all, in_sem.at[1, r]) for r in range(ndp)]

    def ctx_load(p, own_ref, near, dst, sem):
        at = dst.at[pl.ds(p * span, span)]
        here = me == p
        return [
            (here, pltpu.make_async_copy(own_ref, at, sem)),
            (jnp.logical_not(here), pltpu.make_async_copy(near.at[p], at, sem)),
        ]

    l_loads = []
    for p in range(nctx):
        l_loads.append(ctx_load(p, att_own, att_near, right2, l_sem.at[0, p]))
        l_loads.append(ctx_load(p, n1_own.at[p], n1_near, left1, l_sem.at[1, p]))

    def weights(j, slot):
        at = pl.multiple_of(start + j * chunk, chunk)
        return (
            pltpu.make_async_copy(wg_hbm.at[:, pl.ds(at, chunk)], wg_buf.at[slot], w_sem.at[slot, 0]),
            pltpu.make_async_copy(wu_hbm.at[:, pl.ds(at, chunk)], wu_buf.at[slot], w_sem.at[slot, 1]),
            pltpu.make_async_copy(wd_hbm.at[pl.ds(at, chunk)], wd_buf.at[slot], w_sem.at[slot, 2]),
        )

    for copies in n_loads + g_loads:
        go(copies)
    for copy in weights(0, 0):
        copy.start()
    resid_load = pltpu.make_async_copy(resid_hbm, acc, save_sem.at[0])
    resid_load.start()
    for copies in l_loads:
        go(copies)
    dn_got = [x_take.at[2, pl.ds(h * span, span)] for h in range(2)]
    half = width // 2
    dn_copies = [
        remote(
            dn_ref.at[:, pl.ds(h * half, half)], dn_got[h], dn_sem.at[0, h], dn_sem.at[1, h], mate
        )
        for h in range(2)
    ]
    enter(peers + mates(me, y))
    for copy in dn_copies:
        copy.start()

    count = units // chunk
    for copies in n_loads + g_loads:
        done(copies)

    @pl.loop(0, count)
    def _(j):
        slot = j % 2
        for copy in weights(j, slot):
            copy.wait()

        @pl.when(j + 1 < count)
        def _():
            for copy in weights(j + 1, 1 - slot):
                copy.start()

        cols = pl.ds(pl.multiple_of(j * chunk, chunk), chunk)

        @pl.loop(0, tokens // rows)
        def _(i):
            some = pl.ds(pl.multiple_of(i * rows, rows), rows)
            gate = nn(n_all[some], wg_buf[slot])
            up = nn(n_all[some], wu_buf[slot])
            d_act = nt(g_all[some], wd_buf[slot])
            for w, value in enumerate(gate_parts(gate, up, d_act)):
                acts[pl.ds(pl.multiple_of(w * tokens + i * rows, rows), rows), cols] = value

    lefts = (g_all, n_all, n_all)

    def product(w, x, c):
        left = lefts[w]
        block = jnp.concatenate(
            [
                left[:, pl.ds(pl.multiple_of((k * nctx + x * 2 + c) * part, part), part)]
                for k in range(ndp)
            ],
            axis=1,
        )
        return tn(block, acts[w * tokens : (w + 1) * tokens])

    core_copies = [
        remote(give.at[w % 2], take.at[w % 2], core_sem.at[0, w], core_sem.at[1, w], {"ctx": me ^ 1})
        for w in range(3)
    ]
    x_copies = [
        remote(x_give.at[w], x_take.at[w], x_sem.at[0, w], x_sem.at[1, w], {"ctx": me ^ 2})
        for w in range(3)
    ]

    def hand(w):
        give[w % 2, 0] = product(w, 1 - xpos, 1 - core).astype(BF)
        give[w % 2, 1] = product(w, xpos, 1 - core).astype(BF)
        core_copies[w].start()

    def keep(w):
        there = product(w, 1 - xpos, core)
        core_copies[w].wait()
        x_give[w] = (there + take[w % 2, 0].astype(F32)).astype(BF)
        if w < 2:
            x_copies[w].start()
        x_keep[w] = (product(w, xpos, core) + take[w % 2, 1].astype(F32)).astype(BF)

    hand(0)
    keep(0)
    hand(1)
    keep(1)
    hand(2)
    keep(2)

    def z_rows(k):
        return pl.ds(pl.multiple_of(k * part, part), part)

    z_units = pl.ds(pl.multiple_of(start, units), units)

    def landing(w):
        return down_z.at[z] if w == 0 else (gate_z, up_z)[w - 1].at[:, z_units]

    def z_copies(w):
        return [
            remote(
                x_keep.at[w, z_rows(lax.rem(z + s, ndp))],
                landing(w),
                zz_sem.at[0, w, s],
                zz_sem.at[1, w, s],
                peers[s - 1],
            )
            for s in range(1, ndp)
        ]

    def z_own_copy(w):
        return pltpu.make_async_copy(x_keep.at[w, z_rows(z)], landing(w), z_own.at[w])

    def serve(w):
        x_copies[w].wait()
        x_keep[w] = (x_keep[w].astype(F32) + x_take[w].astype(F32)).astype(BF)
        for copy in z_copies(w):
            copy.start()
        z_own_copy(w).start()

    wo, wq = n_all, acts.at[pl.ds(0, width)]
    wk, wv = wg_buf.at[0], wu_buf.at[0]
    loads = [
        pltpu.make_async_copy(src, dst, back_sem.at[i])
        for i, (src, dst) in enumerate(((wo_hbm, wo), (wq_hbm, wq), (wk_hbm, wk), (wv_hbm, wv)))
    ]
    for copy in loads:
        copy.start()
    bias_ref[...] = mask_bias(where_ref[0], where_ref[1], length, span)
    resid_load.wait()
    v = acc[...]
    factor = lax.rsqrt(jnp.mean(v * v, axis=-1, keepdims=True) + EPS)
    for copy in dn_copies:
        copy.wait()
    y_out = remote(out_hbm, out_got, y_sem.at[0, 1], y_sem.at[1, 1], mate)
    y_out.start()
    cols = width // 4

    def dn_part(c):
        return dn_got[c // 2][:, (c % 2) * cols : (c % 2 + 1) * cols]

    dots = jnp.zeros((span, 1), F32)
    for c in range(4):
        at = slice(c * cols, (c + 1) * cols)
        unit = acc[:, at] * factor
        back = dn_ref[:, at].astype(F32) + dn_part(c).astype(F32)
        term = back * unit
        gain_grad_ref[:, at] = jnp.sum(term, axis=0, keepdims=True)
        dots += jnp.sum(term * gain_ref[:, at], axis=-1, keepdims=True)
    dots = dots / width
    for c in range(4):
        at = slice(c * cols, (c + 1) * cols)
        unit = acc[:, at] * factor
        back = dn_ref[:, at].astype(F32) + dn_part(c).astype(F32)
        total = g_all[:span, at].astype(F32) + factor * (back * gain_ref[:, at] - unit * dots)
        acc[:, at] = total
        low[:, at] = total.astype(BF)
    dr_save = pltpu.make_async_copy(acc, dr_out, save_sem.at[1])
    dr_save.start()

    spread = width // nctx

    def low_rows(p):
        return pl.ds(pl.multiple_of(p // 2 * span, span), span)

    def low_cols(p):
        return pl.ds(pl.multiple_of(p % 2 * spread, spread), spread)

    for p in range(nctx):
        for b in range(ndp):
            at = (b * nctx + p) * part
            to = p % 2 * spread + b * part
            give[0, 0, p // 2 * span : (p // 2 + 1) * span, to : to + part] = low[:, at : at + part]
    spreads = [
        remote(
            give.at[0, 0, low_rows(me ^ m), low_cols(me ^ m)],
            left2.at[mine],
            low_sem.at[0, m],
            low_sem.at[1, m],
            {"ctx": me ^ m},
        )
        for m in range(1, nctx)
    ]
    for copy in spreads:
        copy.start()
    left2[mine, :] = give[0, 0, low_rows(me), low_cols(me)]
    loads[0].wait()
    d_att[...] = nt(low[...], wo[...]).astype(BF)
    wide = 128 * group
    heads = wide // HD
    blocks = kvw // 128
    scale = jnp.asarray(HD**-0.5, BF)

    def share(j, m):
        some = pl.ds(pl.multiple_of((me ^ m) * span, span), span)
        return remote(
            dkv.at[j, some], land.at[j, m], dkv_sem.at[0, j, m], dkv_sem.at[1, j, m], {"ctx": me ^ m}
        )

    @pl.loop(0, blocks)
    def _(j):
        lanes = pl.ds(pl.multiple_of(j * wide, 128), wide)
        queries = q_ref[:, lanes] * scale
        grads = d_att[:, lanes]
        keys = kv_ref[:, pl.ds(pl.multiple_of(j * 128, 128), 128)]
        values = kv_ref[:, pl.ds(pl.multiple_of(kvw + j * 128, 128), 128)]
        lse = lse_ref[pl.ds(pl.multiple_of(j * heads, heads), heads), :]
        pair = []
        for h in range(heads):
            at = slice(HD * (h // group), HD * (h // group + 1))
            key, value = keys[:, at], values[:, at]
            query = queries[:, HD * h : HD * (h + 1)]
            grad = grads[:, HD * h : HD * (h + 1)]
            probs = jnp.exp(nt(key, query) + (bias_ref[...] - lse[h : h + 1, :]))
            d_probs = nt(value, grad)
            delta = jnp.sum(probs * d_probs, axis=0, keepdims=True)
            d_scores = (probs * (d_probs - delta)).astype(BF)
            d_value = nn(probs.astype(BF), grad)
            d_key = nn(d_scores, query)
            if h % group == 0:
                sum_key, sum_value = d_key, d_value
            else:
                sum_key, sum_value = sum_key + d_key, sum_value + d_value
            if h % group == group - 1:
                dkv[j, :, at] = sum_key.astype(BF)
                dkv[j, :, slice(128 + at.start, 128 + at.stop)] = sum_value.astype(BF)
            pair.append(tn(key * scale, d_scores))
            if h % 2:
                both = jnp.concatenate(pair, axis=0).T
                turned = both * cos_ref[...] - swap_halves(both) * sin_ref[...]
                right1[mine, pl.ds(pl.multiple_of(j * wide + HD * (h - 1), 128), 128)] = turned.astype(BF)
                pair = []
        for m in range(1, nctx):
            share(j, m).start()

        @pl.when(j == 0)
        def _():
            serve(0)

    loads[1].wait()
    dr_save.wait()
    acc[...] = nt(right1[mine, :qw], wq[...])
    serve(1)
    for j in range(blocks):
        total = dkv[j, mine].astype(F32)
        for m in range(1, nctx):
            share(j, m).wait_recv()
            total += land[j, m].astype(F32)
        d_key = total[:, :128]
        d_key = d_key * cos_ref[...] - swap_halves(d_key) * sin_ref[...]
        right1[mine, qw + 128 * j : qw + 128 * (j + 1)] = d_key.astype(BF)
        right1[mine, qw + kvw + 128 * j : qw + kvw + 128 * (j + 1)] = total[:, 128:].astype(BF)
    own_rows = right1.at[mine]
    r_x = remote(own_rows, own_rows, r_sem.at[0, 0], r_sem.at[1, 0], {"ctx": me ^ 2})
    r_core = remote(own_rows, own_rows, r_sem.at[0, 1], r_sem.at[1, 1], {"ctx": me ^ 1})
    r_onward = remote(
        right1.at[cross], right1.at[cross], r_sem.at[0, 2], r_sem.at[1, 2], {"ctx": me ^ 1}
    )
    r_x.start()
    r_core.start()
    x_copies[2].start()
    loads[2].wait()
    loads[3].wait()
    low[...] = (
        acc[...]
        + nt(right1[mine, qw : qw + kvw], wk[...])
        + nt(right1[mine, qw + kvw :], wv[...])
    ).astype(BF)
    front_save = pltpu.make_async_copy(low, front_out, save_sem.at[2])
    y_front = remote(low, front_got, y_sem.at[0, 0], y_sem.at[1, 0], mate)
    front_save.start()
    y_front.start()

    nq = right1.shape[1]

    def att_copies(w, at):
        return [
            remote(
                prod.at[z_rows(lax.rem(z + s, ndp)), at],
                att_z.at[z, :, at],
                att_sem.at[0, w, s],
                att_sem.at[1, w, s],
                peers[s - 1],
            )
            for s in range(1, ndp)
        ]

    def att_own_copy(w, at):
        return pltpu.make_async_copy(
            prod.at[z_rows(z), at], att_z.at[z, :, at], att_sem.at[0, w, 0]
        )

    out_cols = slice(nq, prod.shape[1])
    qkv_cols = slice(0, nq)
    for copies in l_loads:
        done(copies)
    for copy in spreads:
        copy.wait()
    prod[:, out_cols] = tn(left2[...], right2[...]).astype(BF)
    for copy in att_copies(1, out_cols):
        copy.start()
    att_own_copy(1, out_cols).start()
    r_x.wait_recv()
    r_onward.start()
    r_core.wait_recv()
    r_onward.wait_recv()
    prod[:, qkv_cols] = tn(left1[...], right1[...]).astype(BF)
    for copy in att_copies(0, qkv_cols):
        copy.start()
    att_own_copy(0, qkv_cols).start()
    serve(2)
    for j in range(blocks):
        for m in range(1, nctx):
            share(j, m).wait_send()
    y_out.wait()
    y_front.wait()
    front_save.wait()
    r_x.wait_send()
    r_core.wait_send()
    r_onward.wait_send()
    for w, at in ((1, out_cols), (0, qkv_cols)):
        for copy in att_copies(w, at):
            copy.wait()
        att_own_copy(w, at).wait()
    for w in range(3):
        for copy in z_copies(w):
            copy.wait()
        z_own_copy(w).wait()


def rear(
    where, q, kv, lse, cosine, sine, gain, dn, n2, n_all, og, og_all, og_far, wg, wu, wd,
    wq, wk, wv, wo, resid, n1p, n1_all, att, att_all, out_part, ndp, nctx, chunk=256, rows=256,
):
    span, width = n2.shape
    tokens, length = span * ndp, span * nctx
    units = wg.shape[1] // ndp
    part = width // (ndp * nctx)
    mine = ndp * part
    qw, kvw = wq.shape[1], wk.shape[1]
    qkvw = qw + 2 * kvw
    dma = pltpu.SemaphoreType.DMA
    flat = jax.ShapeDtypeStruct((part, ndp * units), BF)
    row = jax.ShapeDtypeStruct((span, width), BF)
    return pl.pallas_call(
        functools.partial(rear_kernel, ndp, nctx, qw // kvw, chunk, rows),
        in_specs=[SMEM_SPEC] + [VMEM_SPEC] * 7 + [HBM_SPEC] * 18,
        out_specs=[HBM_SPEC] * 8 + [VMEM_SPEC],
        out_shape=[
            jax.ShapeDtypeStruct((ndp, part, units), BF),
            flat,
            flat,
            jax.ShapeDtypeStruct((ndp, part, qkvw + qw), BF),
            row,
            row,
            row,
            jax.ShapeDtypeStruct((span, width), F32),
            jax.ShapeDtypeStruct((1, width), F32),
        ],
        scratch_shapes=[
            pltpu.VMEM((tokens, width), BF),
            pltpu.VMEM((tokens, width), BF),
            pltpu.VMEM((3 * tokens, units), BF),
            pltpu.VMEM((2, width, chunk), BF),
            pltpu.VMEM((2, width, chunk), BF),
            pltpu.VMEM((2, chunk, width), BF),
            pltpu.VMEM((2, 2, mine, units), BF),
            pltpu.VMEM((2, 2, mine, units), BF),
            pltpu.VMEM((3, mine, units), BF),
            pltpu.VMEM((3, mine, units), BF),
            pltpu.VMEM((3, mine, units), BF),
            pltpu.VMEM((length, width // nctx), BF),
            pltpu.VMEM((length, width // nctx), BF),
            pltpu.VMEM((length, qkvw), BF),
            pltpu.VMEM((length, qw), BF),
            pltpu.VMEM((mine, qkvw + qw), BF),
            pltpu.VMEM((span, width), BF),
            pltpu.VMEM((span, qw), BF),
            pltpu.VMEM((length, span), F32),
            pltpu.VMEM((kvw // 128, length, 256), BF),
            pltpu.VMEM((kvw // 128, nctx, span, 256), BF),
            pltpu.VMEM((span, width), F32),
            dma((2, ndp)),
            dma((2, nctx)),
            dma((2, 3)),
            dma((4,)),
            dma((2, 2)),
            dma((2, nctx)),
            dma((2, kvw // 128, nctx)),
            dma((2, 3)),
            dma((2, 3)),
            dma((2, 3)),
            dma((2, 3, ndp)),
            dma((3,)),
            dma((2, 2, ndp)),
            dma((2, 2)),
            dma((3,)),
        ],
        compiler_params=pltpu.CompilerParams(
            vmem_limit_bytes=63 * 1024 * 1024, collective_id=2, has_side_effects=True
        ),
        cost_estimate=cost(12 * tokens * width * units, 4 * tokens * width),
        name="rear",
    )(
        where, q, kv, lse, cosine, sine, gain.reshape(1, width), dn,
        n2, n_all, og, og_all, og_far, wg, wu, wd, wq, wk, wv, wo,
        resid, n1p, n1_all, att, att_all, out_part,
    )


def dot_plain(left, right):
    return jnp.dot(left, right, preferred_element_type=F32)


def dot_right(left, right):
    return lax.dot_general(left, right, (((1,), (1,)), ((), ())), preferred_element_type=F32)


def dot_left(left, right):
    return lax.dot_general(left, right, (((0,), (0,)), ((), ())), preferred_element_type=F32)


def normed(v, gain):
    return v * lax.rsqrt(jnp.mean(v * v, axis=-1, keepdims=True) + EPS) * gain


def norm_back(v, gain, grad):
    factor = lax.rsqrt(jnp.mean(v * v, axis=-1, keepdims=True) + EPS)
    unit = v * factor
    d_unit = grad * gain
    d_gain = jnp.sum(grad * unit, axis=0)
    d_v = factor * (d_unit - unit * jnp.mean(d_unit * unit, axis=-1, keepdims=True))
    return (d_v, d_gain)


def rotate(t, cosine, sine):
    half = t.shape[-1] // 2
    first, second = (t[..., :half], t[..., half:])
    return jnp.concatenate(
        [first * cosine - second * sine, second * cosine + first * sine], axis=-1
    )


def rotate_back(t, cosine, sine):
    half = t.shape[-1] // 2
    first, second = (t[..., :half], t[..., half:])
    return jnp.concatenate(
        [first * cosine + second * sine, second * cosine - first * sine], axis=-1
    )


def score_block(query5, key_all, allowed):
    scores = jnp.einsum(
        "scngd,slnd->sngcl", query5, key_all, preferred_element_type=F32
    ) * HD ** (-0.5)
    return jnp.where(allowed[:, None, None], scores, NEG)


def build(ndp, nctx, nten):
    def pull(v, axis, n, s):
        return lax.ppermute(v, axis, [((i + s) % n, i) for i in range(n)])

    def flip(v, axis, n, bit):
        return lax.ppermute(v, axis, [(i, i ^ bit) for i in range(n)])

    def tensor_sum(v):
        low = v.astype(BF)
        if nten == 2:
            return low.astype(F32) + flip(low, "tensor", 2, 1).astype(F32)
        return lax.psum(low, "tensor").astype(F32)

    def gather_dp(v):
        rows = v.shape[0] // nten
        part = lax.dynamic_slice_in_dim(v, lax.axis_index("tensor") * rows, rows, 0)
        pieces = [v]
        for s in range(1, ndp):
            got = pull(part, "dp", ndp, s)
            pieces.append(got)
            for t in range(1, nten):
                pieces.append(pull(got, "tensor", nten, t))
        return jnp.concatenate(pieces, axis=0)

    def ctx_sum(full):
        r = full.shape[0] // (ndp * nctx)
        me = lax.axis_index("ctx")
        work = full.reshape(ndp, nctx, r, full.shape[1])
        bit = 1
        while bit < nctx:
            left = work.shape[1] // 2
            work = work.reshape(ndp, left, 2, r, full.shape[1])
            mine = (me // bit) % 2
            keep = lax.dynamic_index_in_dim(work, mine, 2, keepdims=False)
            give = lax.dynamic_index_in_dim(work, 1 - mine, 2, keepdims=False)
            got = flip(give, "ctx", nctx, bit)
            work = (keep.astype(F32) + got.astype(F32)).astype(BF)
            bit *= 2
        return work.reshape(ndp, r, full.shape[1])

    def finish_slices(full):
        got = lax.all_to_all(ctx_sum(full), "dp", 0, 0, tiled=True)
        return jnp.swapaxes(got, 0, 1).reshape(got.shape[1], -1).astype(F32)

    def finish_sum(full):
        got = lax.all_to_all(ctx_sum(full), "dp", 0, 0, tiled=True)
        return jnp.sum(got.astype(F32), axis=0)

    def local(
        layer_input,
        output_grad,
        prefix,
        attn_gain,
        w_query,
        w_key,
        w_value,
        w_out,
        mlp_gain,
        w_gate,
        w_up,
        w_down,
    ):
        seqs, span, width = layer_input.shape
        q_heads = w_query.shape[1] // HD
        kv_heads = w_key.shape[1] // HD
        group = q_heads // kv_heads
        zi = lax.axis_index("dp")
        rows = layer_input.astype(F32).reshape(seqs * span, width)
        grad_low = output_grad.reshape(seqs * span, width)
        grad_rows = grad_low.astype(F32)
        grad_all = gather_dp(grad_low)

        first = lax.axis_index("ctx") * span
        position = (first + jnp.arange(span)).astype(F32)
        frequency = ROPE_BASE ** (-jnp.arange(HD // 2).astype(F32) * 2.0 / HD)
        angle = position[:, None] * frequency[None, :]
        cosine = jnp.cos(angle)[None, :, None, :]
        sine = jnp.sin(angle)[None, :, None, :]
        normed1 = normed(rows, attn_gain).astype(BF)
        query = rotate(
            dot_plain(normed1, w_query).reshape(seqs, span, q_heads, HD), cosine, sine
        ).astype(BF)
        keyed = rotate(
            dot_plain(normed1, w_key).reshape(seqs, span, kv_heads, HD), cosine, sine
        ).astype(BF)
        valued = dot_plain(normed1, w_value).astype(BF).reshape(seqs, span, kv_heads * HD)
        key_all, value_all = (
            lax.all_gather(
                keyed.reshape(seqs, span, kv_heads * HD), "ctx", axis=1, tiled=True
            ),
            lax.all_gather(valued, "ctx", axis=1, tiled=True),
        )
        length = key_all.shape[1]
        key_all = key_all.reshape(seqs, length, kv_heads, HD)
        value_all = value_all.reshape(seqs, length, kv_heads, HD)
        query5 = query.reshape(seqs, span, kv_heads, group, HD)
        query_pos = first + jnp.arange(span)
        key_pos = jnp.arange(length)
        allowed = (key_pos[None, None, :] <= query_pos[None, :, None]) | (
            key_pos[None, None, :] < prefix[:, None, None]
        )
        scores = score_block(query5, key_all, allowed)
        top = jnp.max(scores, axis=-1, keepdims=True)
        exponent = jnp.exp(scores - top)
        total = jnp.sum(exponent, axis=-1, keepdims=True)
        log_total = top + jnp.log(total)
        probs_low = (exponent / total).astype(BF)
        attended = jnp.einsum(
            "sngcl,slnd->scngd", probs_low, value_all, preferred_element_type=F32
        )
        attended = attended.astype(BF).reshape(seqs * span, q_heads * HD)
        resid = rows + tensor_sum(dot_plain(attended, w_out))
        normed2 = normed(resid, mlp_gain).astype(BF)
        normed2_all = gather_dp(normed2)
        gate = dot_plain(normed2, w_gate)
        up = dot_plain(normed2, w_up)
        act = (jax.nn.silu(gate) * up).astype(BF)

        def mlp_back(gate, up, d_act):
            sigmoid_gate = jax.nn.sigmoid(gate)
            d_gate_pre = (
                d_act * up * sigmoid_gate * (1.0 + gate * (1.0 - sigmoid_gate))
            ).astype(BF)
            d_up_pre = (d_act * gate * sigmoid_gate).astype(BF)
            return d_gate_pre, d_up_pre

        d_act = dot_right(grad_low, w_down)
        d_gate_pre, d_up_pre = mlp_back(gate, up, d_act)
        back_terms = dot_right(d_gate_pre, w_gate) + dot_right(d_up_pre, w_up)
        d_normed2 = tensor_sum(back_terms)
        output = (resid + tensor_sum(dot_plain(act, w_down))).astype(BF)
        output = output.reshape(seqs, span, width)

        units = w_gate.shape[1] // ndp
        wg = lax.dynamic_slice_in_dim(w_gate, zi * units, units, 1)
        wu = lax.dynamic_slice_in_dim(w_up, zi * units, units, 1)
        wd = lax.dynamic_slice_in_dim(w_down, zi * units, units, 0)
        gate_s = dot_plain(normed2_all, wg)
        up_s = dot_plain(normed2_all, wu)
        d_act_s = dot_right(grad_all, wd)
        act_s = (jax.nn.silu(gate_s) * up_s).astype(BF)
        d_gate_s, d_up_s = mlp_back(gate_s, up_s, d_act_s)
        s_down = finish_slices(dot_left(grad_all, act_s).astype(BF)).T
        s_gate = finish_slices(dot_left(normed2_all, d_gate_s).astype(BF))
        s_up = finish_slices(dot_left(normed2_all, d_up_s).astype(BF))

        d_resid_norm, g_mlp_gain = norm_back(resid, mlp_gain, d_normed2)
        d_resid = grad_rows + d_resid_norm
        d_resid_low = d_resid.astype(BF)
        s_out = finish_sum(dot_left(d_resid_low, attended).astype(BF)).T
        d_attended = dot_right(d_resid_low, w_out).astype(BF).reshape(query5.shape)
        scores = score_block(query5, key_all, allowed)
        probs = jnp.exp(scores - log_total)
        probs_low = probs.astype(BF)
        d_probs = jnp.einsum(
            "scngd,slnd->sngcl", d_attended, value_all, preferred_element_type=F32
        )
        delta = jnp.sum(probs * d_probs, axis=-1, keepdims=True)
        d_scores = (probs * (d_probs - delta)).astype(BF)
        scale = HD ** (-0.5)
        d_query = (
            jnp.einsum("sngcl,slnd->scngd", d_scores, key_all, preferred_element_type=F32) * scale
        )
        d_key_all = (
            jnp.einsum("sngcl,scngd->slnd", d_scores, query5, preferred_element_type=F32) * scale
        )
        d_value_all = jnp.einsum(
            "sngcl,scngd->slnd", probs_low, d_attended, preferred_element_type=F32
        )
        d_kv = jnp.concatenate(
            [
                d_key_all.reshape(length, kv_heads * HD).astype(BF),
                d_value_all.reshape(length, kv_heads * HD).astype(BF),
            ],
            axis=1,
        )
        d_kv = lax.psum_scatter(d_kv, "ctx", scatter_dimension=0, tiled=True).astype(F32)
        d_key, d_val = d_kv[:, : kv_heads * HD], d_kv[:, kv_heads * HD :]
        d_qp = (
            rotate_back(d_query.reshape(seqs, span, q_heads, HD), cosine, sine)
            .astype(BF)
            .reshape(seqs * span, q_heads * HD)
        )
        d_kp = (
            rotate_back(d_key.reshape(seqs, span, kv_heads, HD), cosine, sine)
            .astype(BF)
            .reshape(seqs * span, kv_heads * HD)
        )
        d_vp = d_val.astype(BF).reshape(seqs * span, kv_heads * HD)
        front_terms = dot_right(d_qp, w_query) + dot_right(d_kp, w_key) + dot_right(d_vp, w_value)
        d_normed1 = tensor_sum(front_terms)
        d_rows_norm, g_attn_gain = norm_back(rows, attn_gain, d_normed1)
        d_input = d_resid + d_rows_norm
        d_input = d_input.reshape(seqs, span, width)
        s_qkv = finish_sum(
            dot_left(normed1, jnp.concatenate([d_qp, d_kp, d_vp], axis=1)).astype(BF)
        )
        nq, nk = q_heads * HD, kv_heads * HD
        s_query, s_key, s_value = s_qkv[:, :nq], s_qkv[:, nq : nq + nk], s_qkv[:, nq + nk :]
        gains = jnp.stack([g_attn_gain, g_mlp_gain])
        gains = lax.psum_scatter(gains, ("dp", "ctx"), scatter_dimension=1, tiled=True)
        return (
            output,
            d_input,
            gains[0],
            s_query,
            s_key,
            s_value,
            s_out,
            gains[1],
            s_gate,
            s_up,
            s_down,
        )

    return local


def suits(ndp, nctx, nten, layer_input, output_grad, prefix, attn_gain, w_query, w_key, w_value, w_out, mlp_gain, w_gate, w_up, w_down):
    seqs, span, width = layer_input.shape
    return (
        seqs == 1
        and (ndp, nctx, nten) == (4, 4, 2)
        and (span, width) == (256, 2048)
        and (w_query.shape[1], w_key.shape[1], w_gate.shape[1]) == (1024, 256, 4096)
    )


def build_fast(ndp, nctx, nten):
    def local(
        layer_input,
        output_grad,
        prefix,
        attn_gain,
        w_query,
        w_key,
        w_value,
        w_out,
        mlp_gain,
        w_gate,
        w_up,
        w_down,
    ):
        seqs, span, width = layer_input.shape
        kvw, nq = w_key.shape[1], w_query.shape[1]
        low = layer_input.reshape(span, width)
        grad_low = output_grad.reshape(span, width)
        first = lax.axis_index("ctx") * span
        where = jnp.stack([first, prefix[0]]).astype(jnp.int32)
        cosine, sine = rope_tables(first, span)
        n1p, query, kv, attended, lse, resid, normed2, grad_all = front(
            where, low, attn_gain, w_query, w_key, w_value, w_out, cosine, sine, mlp_gain, grad_low, ndp, nctx
        )
        out_part, dn, n_all, n1_all, att_all, grad_far = middle(
            normed2, grad_low, w_gate, w_up, w_down, n1p, attended, grad_all, ndp, nctx
        )
        down_z, gate_z, up_z, att_z, front_part, front_got, out_got, d_resid, g_mlp_gain = rear(
            where, query, kv, lse, cosine, sine, mlp_gain, dn, normed2, n_all, grad_low, grad_all, grad_far,
            w_gate, w_up, w_down, w_query, w_key, w_value, w_out, resid, n1p, n1_all, attended, att_all,
            out_part, ndp, nctx,
        )
        output = resid + (out_part.astype(F32) + out_got.astype(F32))
        output = output.astype(BF).reshape(seqs, span, width)
        s_down = jnp.swapaxes(down_z, 1, 2).reshape(w_down.shape[0], -1).astype(F32)
        s_gate, s_up = gate_z.astype(F32), up_z.astype(F32)
        s_att = jnp.sum(att_z.astype(F32), axis=0)
        s_query, s_key = s_att[:, :nq], s_att[:, nq : nq + kvw]
        s_value, s_out = s_att[:, nq + kvw : nq + 2 * kvw], s_att[:, nq + 2 * kvw :].T
        d_normed1 = front_part.astype(F32) + front_got.astype(F32)
        d_rows_norm, g_attn_gain = norm_back(low.astype(F32), attn_gain, d_normed1)
        d_input = (d_resid + d_rows_norm).reshape(seqs, span, width)
        gains = jnp.stack([g_attn_gain, g_mlp_gain[0]])
        gains = jnp.swapaxes(gains.reshape(2, ndp * nctx, -1), 0, 1)
        gains = lax.all_to_all(gains, ("dp", "ctx"), 0, 0, tiled=True)
        gains = jnp.sum(gains, axis=0)
        return (
            output,
            d_input,
            gains[0],
            s_query,
            s_key,
            s_value,
            s_out,
            gains[1],
            s_gate,
            s_up,
            s_down,
        )

    return local


def solution(mesh):
    sizes = mesh.shape["dp"], mesh.shape["ctx"], mesh.shape["tensor"]
    plain, fast = build(*sizes), build_fast(*sizes)

    def local(*args):
        return (fast if suits(*sizes, *args) else plain)(*args)

    return jax.shard_map(
        local,
        mesh=mesh,
        in_specs=(
            P("dp", "ctx", None),
            P("dp", "ctx", None),
            P("dp"),
            P(),
            P(None, "tensor"),
            P(None, "tensor"),
            P(None, "tensor"),
            P("tensor", None),
            P(),
            P(None, "tensor"),
            P(None, "tensor"),
            P("tensor", None),
        ),
        out_specs=(
            P("dp", "ctx", None),
            P("dp", "ctx", None),
            P(("dp", "ctx")),
            P(("dp", "ctx"), "tensor"),
            P(("dp", "ctx"), "tensor"),
            P(("dp", "ctx"), "tensor"),
            P("tensor", ("dp", "ctx")),
            P(("dp", "ctx")),
            P(("dp", "ctx"), "tensor"),
            P(("dp", "ctx"), "tensor"),
            P("tensor", ("dp", "ctx")),
        ),
        check_vma=False,
    )
```

profile of v0, /device:TPU:25, one launch (start us, length us, event | category | flops | bytes accessed | tf_op | source)
XLA Modules:
  0.0 349.9 jit_solution(7091040290147065291)
XLA Ops:
  1.3 1.5 fusion.9
  2.8 0.5 fusion.12
  3.4 0.6 pad_add_fusion.where_ref
  4.0 1.0 pad_maximum_fusion
  5.0 54.0 %front.1 = (bf16[4,256,512]{2,1,0:T(8,128)(2,1)}, bf16[256,1024]{1,0:T(8,128)(2,1)}, bf16[1024,512]{1,0:T(8,128)(2,1)}, bf16[256,1024]{1,0:T(8,128)(2,1)}, f32[1...) custom-call(s32[2]{0:T(128)} %pad_add_fusion.where_ref, ...), custom_call_target="tpu_custom_call" | custom-call | flops 2684354560 | bytes 10485760 | tf_op jit(solution)/shard_map/front/pallas_call | solution.py:269
  59.0 76.3 %middle.1 = (bf16[256,2048]{1,0:T(8,128)(2,1)}, bf16[256,2048]{1,0:T(8,128)(2,1)}, bf16[4,256,2048]{2,1,0:T(8,128)(2,1)}, bf16[4,256,512]{2,1,0:T(8,128)(2,1)}, ...) custom-call(bf16[256,2048]{1,0:T(8,128)(2,1)} %get-tuple-element.35.n_ref.n_hbm.n_own, ...), custom_call_target="tpu_custom_call" | custom-call | flops 25769803776 | bytes 50331648 | tf_op jit(solution)/shard_map/middle/pallas_call | solution.py:481
  135.3 0.0 copy-start.9
  135.3 187.2 %rear.1 = (bf16[4,128,1024]{2,1,0:T(8,128)(2,1)}, bf16[128,4096]{1,0:T(8,128)(2,1)}, bf16[128,4096]{1,0:T(8,128)(2,1)}, bf16[4,128,2560]{2,1,0:T(8,128)(2,1)}, b...) custom-call(s32[2]{0:T(128)} %pad_add_fusion.where_ref, ...), custom_call_target="tpu_custom_call" | custom-call | flops 25769803776 | bytes 8388608 | tf_op jit(solution)/shard_map/rear/pallas_call | solution.py:926
  322.5 0.0 copy-start.10
  322.5 0.0 copy-start.8
  322.5 0.0 copy-done.9
  322.6 2.8 fusion.8
  325.4 0.6 maximum_bitcast_fusion
  326.0 6.7 %all-to-all-start = ((f32[16,2,128]{2,1,0:T(2,128)}), f32[16,2,128]{2,1,0:T(2,128)S(1)}, u32[]{:S(2)}, u32[]{:S(2)}) async-start(f32[16,2,128]{2,1,0:T(2,128)} %maximum_bitcast_fusion), calls=%async_computation | async-start | bytes 32768 | tf_op jit(solution)/shard_map/all_to_all | solution.py:1313
  332.7 0.2 convert_bitcast_fusion
  333.0 0.0 copy-start.4
  333.0 0.0 copy-start.6
  333.0 0.0 copy-start.7
  333.0 2.4 convert_reduce_fusion
  335.4 0.9 slice_bitcast_fusion
  336.4 1.4 fusion.11
  337.8 0.3 copy-done.1
  338.1 0.4 copy-done.2
  338.6 0.7 copy-done.3
  339.3 2.1 fusion.7
  341.3 0.7 fusion.13
  342.0 1.8 copy.35
  343.8 1.0 copy.36
  344.8 2.8 convert_element_type.59
  347.6 1.5 convert_element_type.60
  349.1 0.0 all-to-all-done
  349.2 0.5 slice_bitcast_fusion.1
  (17 shorter events, 0.1 us)
Async XLA Ops:
  135.3 187.3 %copy-start.9 = (f32[2048]{0:T(1024)S(1)}, f32[2048]{0:T(1024)}, u32[]{:S(2)}) copy-start(f32[2048]{0:T(1024)} %param.15) | copy-start | bytes 24580
  322.5 2.9 copy-start.10
  322.5 10.2 %copy-start.8 = (bf16[4,128,1024]{2,1,0:T(8,128)(2,1)S(1)}, bf16[4,128,1024]{2,1,0:T(8,128)(2,1)}, u32[]{:S(2)}) copy-start(bf16[4,128,1024]{2,1,0:T(8,128)(2,1)} %get-tuple-element.56) | copy-start | bytes 3145732
  326.0 23.1 %all-to-all-start = ((f32[16,2,128]{2,1,0:T(2,128)}), f32[16,2,128]{2,1,0:T(2,128)S(1)}, u32[]{:S(2)}, u32[]{:S(2)}) async-start(f32[16,2,128]{2,1,0:T(2,128)} %maximum_bitcast_fusion), calls=%async_computation | async-start | bytes 32768 | tf_op jit(solution)/shard_map/all_to_all | solution.py:1313
  333.0 3.3 copy-start.4
  333.0 3.3 copy-start.6
  333.0 3.3 copy-start.7
  336.3 1.5 copy-start
  336.3 1.8 copy-start.1
  336.3 2.2 copy-start.2
  336.3 2.9 copy-start.3
  343.8 3.8 %copy-start.5 = (bf16[128,4096]{1,0:T(8,128)(2,1)S(1)}, bf16[128,4096]{1,0:T(8,128)(2,1)}, u32[]{:S(2)}) copy-start(bf16[128,4096]{1,0:T(8,128)(2,1)} %get-tuple-element.55) | copy-start | bytes 3145732
where the time goes:
time: 355 us; the launch traced here: 350 us
  Pallas kernels  318 us (90%)
  other arithmetic  17.6 us (5%)
  starting transfers between devices  6.71 us (2%)
  local copies, waits for them, and re-layouts  6.41 us (2%)
    pallas_call x1, Pallas kernels, rear(): pl.pallas_call(functools.partial(rear_kernel, ndp, nctx, qw // kvw, chunk...  187 us
    pallas_call x1, Pallas kernels, middle(): pl.pallas_call(functools.partial(middle_kernel, ndp, nctx), grid=(units /...  76.3 us
    pallas_call x1, Pallas kernels, front(): pl.pallas_call(functools.partial(front_kernel, ndp, nctx, group), in_spec...  54 us
  transfers between devices with their start and end apart: 1, of which 0 were waited for; matrix products, arithmetic and copies ran while one was open for 4% of the time, Pallas kernels for 0%

commit v1 on v0

--- a/solution.py
+++ b/solution.py
@@ -308,33 +308,18 @@
 
 class Far:
     def __init__(self, z, y, blocks, far, sems):
-        self.z, self.far = z, far
         rows = halves(y, far.shape[0])
         block = jnp.where(z == 1, 3, 0)
         to = jnp.where(z == 1, 0, 3)
-        self.over = remote(
-            blocks.at[block, rows], far.at[rows], sems.at[0, 0], sems.at[1, 0], {"dp": to}
-        )
-        self.swap = remote(
-            far.at[rows], far.at[rows], sems.at[0, 1], sems.at[1, 1], {"tensor": 1 - y}
-        )
+        self.over = remote(blocks.at[block, rows], far.at[rows], sems.at[0], sems.at[1], {"dp": to})
         self.gives = (z == 1) | (z == 2)
         self.takes = (z == 0) | (z == 3)
 
     def start(self):
         pl.when(self.gives)(lambda: self.over.start())
 
-    def onward(self):
-        @pl.when(self.takes)
-        def _():
-            self.over.wait_recv()
-            self.swap.start()
-
-    def wait_recv(self):
-        pl.when(self.takes)(lambda: self.swap.wait_recv())
-
     def finish(self):
-        pl.when(self.takes)(lambda: self.swap.wait_send())
+        pl.when(self.takes)(lambda: self.over.wait_recv())
         pl.when(self.gives)(lambda: self.over.wait_send())
 
 
@@ -431,7 +416,6 @@
     def _():
         enter(around(z, ndp) + mates(me, y))
         gather.send(1)
-        far.start()
         for copy in spreads:
             copy.start()
 
@@ -458,7 +442,7 @@
     @pl.when(j == 5)
     def _():
         gather.step(2)
-        far.onward()
+        far.start()
 
     @pl.when(j == last)
     def _():
@@ -467,7 +451,6 @@
         dn_ref[...] = dn_acc[...].astype(BF)
         for copy in spreads:
             copy.wait()
-        far.wait_recv()
         far.finish()
         gather.finish()
 
@@ -501,7 +484,7 @@
             dma((ndp - 1, 2, 2)),
             dma((2, nctx)),
             dma((2, nctx)),
-            dma((2, 2)),
+            dma((2,)),
         ],
         compiler_params=own(1),
         cost_estimate=cost(12 * span * width * units, 6 * width * units),
@@ -518,7 +501,7 @@
     n_all, g_all, acts, wg_buf, wu_buf, wd_buf, give, take, x_give, x_take, x_keep,
     left1, left2, right1, right2, prod, low, d_att, bias_ref, dkv, land, acc,
     in_sem, l_sem, w_sem, back_sem, dn_sem, low_sem, dkv_sem, r_sem, core_sem, x_sem, zz_sem, z_own,
-    att_sem, y_sem, save_sem,
+    att_sem, y_sem, save_sem, far_sem,
 ):
     z, me, y = lax.axis_index("dp"), lax.axis_index("ctx"), lax.axis_index("tensor")
     tokens, width = n_all.shape
@@ -534,18 +517,10 @@
     mine = pl.ds(pl.multiple_of(me * span, span), span)
     cross = pl.ds(pl.multiple_of((me ^ 2) * span, span), span)
 
-    def block_load(r, own_ref, near, far, dst, sem):
+    def block_load(r, own_ref, near, dst, sem):
         block = lax.rem(jnp.where(z < ndp // 2, z + r, z + ndp - r), ndp)
         at = dst.at[pl.ds(r * span, span)]
-        if r == 0:
-            return [(None, pltpu.make_async_copy(own_ref, at, sem))]
-        if r < ndp - 1 or far is None:
-            return [(None, pltpu.make_async_copy(near.at[block], at, sem))]
-        end = (z == 0) | (z == ndp - 1)
-        return [
-            (end, pltpu.make_async_copy(far, at, sem)),
-            (jnp.logical_not(end), pltpu.make_async_copy(near.at[block], at, sem)),
-        ]
+        return pltpu.make_async_copy(own_ref if r == 0 else near.at[block], at, sem)
 
     def go(copies):
         for ok, copy in copies:
@@ -557,8 +532,14 @@
     def done(copies):
         copies[0][1].wait()
 
-    n_loads = [block_load(r, n_own, n_near, None, n_all, in_sem.at[0, r]) for r in range(ndp)]
-    g_loads = [block_load(r, g_own, g_near, g_far, g_all, in_sem.at[1, r]) for r in range(ndp)]
+    n_loads = [block_load(r, n_own, n_near, n_all, in_sem.at[0, r]) for r in range(ndp)]
+    g_loads = [block_load(r, g_own, g_near, g_all, in_sem.at[1, r]) for r in range(ndp)]
+    end = (z == 0) | (z == ndp - 1)
+    tail = ndp - 1
+    half_rows = halves(y, span)
+    half_at = g_all.at[pl.ds(pl.multiple_of(tail * span + y * (span // 2), span // 2), span // 2)]
+    half_load = pltpu.make_async_copy(g_far.at[half_rows], half_at, in_sem.at[1, tail])
+    half_swap = remote(g_far.at[half_rows], half_at, far_sem.at[0], far_sem.at[1], mate)
 
     def ctx_load(p, own_ref, near, dst, sem):
         at = dst.at[pl.ds(p * span, span)]
@@ -581,8 +562,10 @@
             pltpu.make_async_copy(wd_hbm.at[pl.ds(at, chunk)], wd_buf.at[slot], w_sem.at[slot, 2]),
         )
 
-    for copies in n_loads + g_loads:
-        go(copies)
+    for copy in n_loads + g_loads[:tail]:
+        copy.start()
+    pl.when(end)(lambda: half_load.start())
+    pl.when(jnp.logical_not(end))(lambda: g_loads[tail].start())
     for copy in weights(0, 0):
         copy.start()
     resid_load = pltpu.make_async_copy(resid_hbm, acc, save_sem.at[0])
@@ -598,12 +581,13 @@
         for h in range(2)
     ]
     enter(peers + mates(me, y))
+    pl.when(end)(lambda: half_swap.start())
     for copy in dn_copies:
         copy.start()
 
     count = units // chunk
-    for copies in n_loads + g_loads:
-        done(copies)
+    for copy in n_loads + g_loads[:tail]:
+        copy.wait()
 
     @pl.loop(0, count)
     def _(j):
@@ -620,6 +604,15 @@
 
         @pl.loop(0, tokens // rows)
         def _(i):
+            @pl.when((j == 0) & (i == tail))
+            def _():
+                pl.when(jnp.logical_not(end))(lambda: g_loads[tail].wait())
+
+                @pl.when(end)
+                def _():
+                    half_load.wait()
+                    half_swap.wait()
+
             some = pl.ds(pl.multiple_of(i * rows, rows), rows)
             gate = nn(n_all[some], wg_buf[slot])
             up = nn(n_all[some], wu_buf[slot])
@@ -976,6 +969,7 @@
             dma((2, 2, ndp)),
             dma((2, 2)),
             dma((3,)),
+            dma((2,)),
         ],
         compiler_params=pltpu.CompilerParams(
             vmem_limit_bytes=63 * 1024 * 1024, collective_id=2, has_side_effects=True

time: 355 us -> 343 us (0.966)
  Pallas kernels: 318 us -> 307 us
    pallas_call x1, Pallas kernels: 76.3 us -> 59.3 us  [middle(): pl.pallas_call(functools.partial(middle_kernel, ndp, nctx), grid=(units /...]
    pallas_call x1, Pallas kernels: 187 us -> 194 us  [rear(): pl.pallas_call(functools.partial(rear_kernel, ndp, nctx, qw // kvw, chunk...]
where the time goes in v1:
time: 343 us; the launch traced here: 338 us
  Pallas kernels  307 us (90%)
  other arithmetic  17.6 us (5%)
  local copies, waits for them, and re-layouts  6.41 us (2%)
  starting transfers between devices  5.67 us (2%)
    pallas_call x1, Pallas kernels, rear(): pl.pallas_call(functools.partial(rear_kernel, ndp, nctx, qw // kvw, chunk...  194 us
    pallas_call x1, Pallas kernels, middle(): pl.pallas_call(functools.partial(middle_kernel, ndp, nctx), grid=(units /...  59.3 us
    pallas_call x1, Pallas kernels, front(): pl.pallas_call(functools.partial(front_kernel, ndp, nctx, group), in_spec...  54 us
  transfers between devices with their start and end apart: 1, of which 0 were waited for; matrix products, arithmetic and copies ran while one was open for 4% of the time, Pallas kernels for 0%

profile of v1, /device:TPU:25, one launch (start us, length us, event | category | flops | bytes accessed | tf_op | source)
XLA Modules:
  0.0 338.1 jit_solution(11490374594305456330)
XLA Ops:
  1.3 1.5 fusion.9
  2.8 0.5 fusion.12
  3.4 0.6 pad_add_fusion.where_ref
  4.0 1.0 pad_maximum_fusion
  5.0 54.0 %front.1 = (bf16[4,256,512]{2,1,0:T(8,128)(2,1)}, bf16[256,1024]{1,0:T(8,128)(2,1)}, bf16[1024,512]{1,0:T(8,128)(2,1)}, bf16[256,1024]{1,0:T(8,128)(2,1)}, f32[1...) custom-call(s32[2]{0:T(128)} %pad_add_fusion.where_ref, ...), custom_call_target="tpu_custom_call" | custom-call | flops 2684354560 | bytes 10485760 | tf_op jit(solution)/shard_map/front/pallas_call | solution.py:269
  59.0 59.3 %middle.1 = (bf16[256,2048]{1,0:T(8,128)(2,1)}, bf16[256,2048]{1,0:T(8,128)(2,1)}, bf16[4,256,2048]{2,1,0:T(8,128)(2,1)}, bf16[4,256,512]{2,1,0:T(8,128)(2,1)}, ...) custom-call(bf16[256,2048]{1,0:T(8,128)(2,1)} %get-tuple-element.35.n_ref.n_hbm.n_own, ...), custom_call_target="tpu_custom_call" | custom-call | flops 25769803776 | bytes 50331648 | tf_op jit(solution)/shard_map/middle/pallas_call | solution.py:464
  118.2 0.0 copy-start.9
  118.2 193.6 %rear.1 = (bf16[4,128,1024]{2,1,0:T(8,128)(2,1)}, bf16[128,4096]{1,0:T(8,128)(2,1)}, bf16[128,4096]{1,0:T(8,128)(2,1)}, bf16[4,128,2560]{2,1,0:T(8,128)(2,1)}, b...) custom-call(s32[2]{0:T(128)} %pad_add_fusion.where_ref, ...), custom_call_target="tpu_custom_call" | custom-call | flops 25769803776 | bytes 8388608 | tf_op jit(solution)/shard_map/rear/pallas_call | solution.py:919
  311.8 0.0 copy-start.10
  311.8 0.0 copy-start.8
  311.8 0.0 copy-done.9
  311.9 2.8 fusion.8
  314.7 0.0 copy-done.10
  314.7 0.6 maximum_bitcast_fusion
  315.3 5.7 %all-to-all-start = ((f32[16,2,128]{2,1,0:T(2,128)}), f32[16,2,128]{2,1,0:T(2,128)S(1)}, u32[]{:S(2)}, u32[]{:S(2)}) async-start(f32[16,2,128]{2,1,0:T(2,128)} %maximum_bitcast_fusion), calls=%async_computation | async-start | bytes 32768 | tf_op jit(solution)/shard_map/all_to_all | solution.py:1307
  321.0 0.2 convert_bitcast_fusion
  321.2 0.0 copy-start.4
  321.2 0.0 copy-start.6
  321.3 2.4 convert_reduce_fusion
  323.7 0.9 slice_bitcast_fusion
  324.6 1.4 fusion.11
  326.1 0.3 copy-done.1
  326.4 0.4 copy-done.2
  326.8 0.7 copy-done.3
  327.5 2.1 fusion.7
  329.6 0.7 fusion.13
  330.3 1.8 copy.35
  332.1 1.0 copy.36
  333.1 2.8 convert_element_type.59
  335.9 1.5 convert_element_type.60
  337.4 0.0 all-to-all-done
  337.4 0.5 slice_bitcast_fusion.1
  (17 shorter events, 0.1 us)
Async XLA Ops:
  118.2 193.6 %copy-start.9 = (f32[2048]{0:T(1024)S(1)}, f32[2048]{0:T(1024)}, u32[]{:S(2)}) copy-start(f32[2048]{0:T(1024)} %param.15) | copy-start | bytes 24580
  311.8 2.9 copy-start.10
  311.8 9.1 %copy-start.8 = (bf16[4,128,1024]{2,1,0:T(8,128)(2,1)S(1)}, bf16[4,128,1024]{2,1,0:T(8,128)(2,1)}, u32[]{:S(2)}) copy-start(bf16[4,128,1024]{2,1,0:T(8,128)(2,1)} %get-tuple-element.56) | copy-start | bytes 3145732
  315.3 22.1 %all-to-all-start = ((f32[16,2,128]{2,1,0:T(2,128)}), f32[16,2,128]{2,1,0:T(2,128)S(1)}, u32[]{:S(2)}, u32[]{:S(2)}) async-start(f32[16,2,128]{2,1,0:T(2,128)} %maximum_bitcast_fusion), calls=%async_computation | async-start | bytes 32768 | tf_op jit(solution)/shard_map/all_to_all | solution.py:1307
  321.2 3.3 copy-start.4
  321.2 3.3 copy-start.6
  321.2 3.3 copy-start.7
  324.6 1.5 copy-start
  324.6 1.8 copy-start.1
  324.6 2.2 copy-start.2
  324.6 2.9 copy-start.3
  332.1 3.8 %copy-start.5 = (bf16[128,4096]{1,0:T(8,128)(2,1)S(1)}, bf16[128,4096]{1,0:T(8,128)(2,1)}, u32[]{:S(2)}) copy-start(bf16[128,4096]{1,0:T(8,128)(2,1)} %get-tuple-element.55) | copy-start | bytes 3145732

commit v2 on v1

--- a/solution.py
+++ b/solution.py
@@ -494,14 +494,15 @@
 
 def rear_kernel(
     ndp, nctx, group, chunk, rows,
-    where_ref, q_ref, kv_ref, lse_ref, cos_ref, sin_ref, gain_ref, dn_ref,
+    where_ref, q_ref, kv_ref, lse_ref, cos_ref, sin_ref, gain_ref, gain1_ref, dn_ref,
     n_own, n_near, g_own, g_near, g_far, wg_hbm, wu_hbm, wd_hbm, wq_hbm, wk_hbm, wv_hbm, wo_hbm,
-    resid_hbm, n1_own, n1_near, att_own, att_near, out_hbm,
-    down_z, gate_z, up_z, att_z, front_out, front_got, out_got, dr_out, gain_grad_ref,
+    resid_hbm, n1_own, n1_near, att_own, att_near, out_hbm, x_hbm,
+    down_z, gate_z, up_z, att_z, front_got, out_got, dr_out, output, input_grad, gains_ref,
     n_all, g_all, acts, wg_buf, wu_buf, wd_buf, give, take, x_give, x_take, x_keep,
     left1, left2, right1, right2, prod, low, d_att, bias_ref, dkv, land, acc,
+    gain_grad_ref, gains, gains_x, gains_z,
     in_sem, l_sem, w_sem, back_sem, dn_sem, low_sem, dkv_sem, r_sem, core_sem, x_sem, zz_sem, z_own,
-    att_sem, y_sem, save_sem, far_sem,
+    att_sem, y_sem, save_sem, far_sem, tail_sem, gx_sem, gz_sem,
 ):
     z, me, y = lax.axis_index("dp"), lax.axis_index("ctx"), lax.axis_index("tensor")
     tokens, width = n_all.shape
@@ -840,9 +841,7 @@
         + nt(right1[mine, qw : qw + kvw], wk[...])
         + nt(right1[mine, qw + kvw :], wv[...])
     ).astype(BF)
-    front_save = pltpu.make_async_copy(low, front_out, save_sem.at[2])
     y_front = remote(low, front_got, y_sem.at[0, 0], y_sem.at[1, 0], mate)
-    front_save.start()
     y_front.start()
 
     nq = right1.shape[1]
@@ -882,13 +881,94 @@
     for copy in att_copies(0, qkv_cols):
         copy.start()
     att_own_copy(0, qkv_cols).start()
+
+    room = [n_all.at[pl.ds(i * span, span)] for i in range(4)]
+
+    def fetch(src, dst, i):
+        return pltpu.make_async_copy(src, dst, tail_sem.at[i])
+
+    first = [fetch(resid_hbm, acc, 0), fetch(out_hbm, room[0], 1), fetch(x_hbm, room[1], 2)]
+    for copy in first:
+        copy.start()
+    y_out.wait()
+    got = fetch(out_got, room[2], 3)
+    got.start()
+    for copy in first + [got]:
+        copy.wait()
+    g_all[:span] = (
+        acc[...] + (n_all[:span].astype(F32) + n_all[2 * span : 3 * span].astype(F32))
+    ).astype(BF)
+    out_save = pltpu.make_async_copy(g_all.at[pl.ds(0, span)], output, tail_sem.at[4])
+    out_save.start()
+    y_front.wait()
+    last = [fetch(dr_out, acc, 5), fetch(front_got, room[3], 6)]
+    for copy in last:
+        copy.start()
+    for copy in last:
+        copy.wait()
+    v = n_all[span : 2 * span].astype(F32)
+    factor = lax.rsqrt(jnp.mean(v * v, axis=-1, keepdims=True) + EPS)
+
+    def front_part(at):
+        x = n_all[span : 2 * span, at].astype(F32)
+        return x * factor, low[:, at].astype(F32) + n_all[3 * span :, at].astype(F32)
+
+    gains[...] = jnp.zeros(gains.shape, F32)
+    dots = jnp.zeros((span, 1), F32)
+    for c in range(ndp):
+        at = slice(c * cols, (c + 1) * cols)
+        unit, back = front_part(at)
+        term = back * unit
+        row = jnp.sum(term, axis=0, keepdims=True)
+        for p in range(nctx):
+            some = slice(p * part, (p + 1) * part)
+            gains[p, 0:1, c * part : (c + 1) * part] = row[:, some]
+            gains[p, 1:2, c * part : (c + 1) * part] = gain_grad_ref[
+                :, c * cols + p * part : c * cols + (p + 1) * part
+            ]
+        dots += jnp.sum(term * gain1_ref[:, at], axis=-1, keepdims=True)
+    dots = dots / width
+    gx_copies = [
+        remote(gains.at[me ^ m], gains_x.at[m], gx_sem.at[0, m], gx_sem.at[1, m], {"ctx": me ^ m})
+        for m in range(1, nctx)
+    ]
+    for copy in gx_copies:
+        copy.start()
+    for c in range(4):
+        at = slice(c * cols, (c + 1) * cols)
+        unit, back = front_part(at)
+        acc[:, at] += factor * (back * gain1_ref[:, at] - unit * dots)
+    grad_save = pltpu.make_async_copy(acc, input_grad, tail_sem.at[7])
+    grad_save.start()
+    total = gains[me]
+    for m in range(1, nctx):
+        gx_copies[m - 1].wait()
+        total += gains_x[m]
+    for b in range(ndp):
+        gains_z[0, b] = total[:, b * part : (b + 1) * part]
+    gz_copies = [
+        remote(
+            gains_z.at[0, lax.rem(z + s, ndp)],
+            gains_z.at[1, s],
+            gz_sem.at[0, s],
+            gz_sem.at[1, s],
+            peers[s - 1],
+        )
+        for s in range(1, ndp)
+    ]
+    for copy in gz_copies:
+        copy.start()
     serve(2)
+    total = gains_z[0, z]
+    for s in range(1, ndp):
+        gz_copies[s - 1].wait()
+        total += gains_z[1, s]
+    gains_ref[...] = total
+    out_save.wait()
+    grad_save.wait()
     for j in range(blocks):
         for m in range(1, nctx):
             share(j, m).wait_send()
-    y_out.wait()
-    y_front.wait()
-    front_save.wait()
     r_x.wait_send()
     r_core.wait_send()
     r_onward.wait_send()
@@ -903,8 +983,8 @@
 
 
 def rear(
-    where, q, kv, lse, cosine, sine, gain, dn, n2, n_all, og, og_all, og_far, wg, wu, wd,
-    wq, wk, wv, wo, resid, n1p, n1_all, att, att_all, out_part, ndp, nctx, chunk=256, rows=256,
+    where, q, kv, lse, cosine, sine, gain, gain1, dn, n2, n_all, og, og_all, og_far, wg, wu, wd,
+    wq, wk, wv, wo, resid, n1p, n1_all, att, att_all, out_part, x, ndp, nctx, chunk=256, rows=256,
 ):
     span, width = n2.shape
     tokens, length = span * ndp, span * nctx
@@ -918,8 +998,8 @@
     row = jax.ShapeDtypeStruct((span, width), BF)
     return pl.pallas_call(
         functools.partial(rear_kernel, ndp, nctx, qw // kvw, chunk, rows),
-        in_specs=[SMEM_SPEC] + [VMEM_SPEC] * 7 + [HBM_SPEC] * 18,
-        out_specs=[HBM_SPEC] * 8 + [VMEM_SPEC],
+        in_specs=[SMEM_SPEC] + [VMEM_SPEC] * 8 + [HBM_SPEC] * 19,
+        out_specs=[HBM_SPEC] * 9 + [VMEM_SPEC],
         out_shape=[
             jax.ShapeDtypeStruct((ndp, part, units), BF),
             flat,
@@ -927,9 +1007,10 @@
             jax.ShapeDtypeStruct((ndp, part, qkvw + qw), BF),
             row,
             row,
+            jax.ShapeDtypeStruct((span, width), F32),
             row,
             jax.ShapeDtypeStruct((span, width), F32),
-            jax.ShapeDtypeStruct((1, width), F32),
+            jax.ShapeDtypeStruct((8, part), F32),
         ],
         scratch_shapes=[
             pltpu.VMEM((tokens, width), BF),
@@ -954,6 +1035,10 @@
             pltpu.VMEM((kvw // 128, length, 256), BF),
             pltpu.VMEM((kvw // 128, nctx, span, 256), BF),
             pltpu.VMEM((span, width), F32),
+            pltpu.VMEM((1, width), F32),
+            pltpu.VMEM((nctx, 8, ndp * part), F32),
+            pltpu.VMEM((nctx, 8, ndp * part), F32),
+            pltpu.VMEM((2, ndp, 8, part), F32),
             dma((2, ndp)),
             dma((2, nctx)),
             dma((2, 3)),
@@ -970,16 +1055,19 @@
             dma((2, 2)),
             dma((3,)),
             dma((2,)),
+            dma((8,)),
+            dma((2, nctx)),
+            dma((2, ndp)),
         ],
         compiler_params=pltpu.CompilerParams(
-            vmem_limit_bytes=63 * 1024 * 1024, collective_id=2, has_side_effects=True
+            vmem_limit_bytes=127 * 512 * 1024, collective_id=2, has_side_effects=True
         ),
         cost_estimate=cost(12 * tokens * width * units, 4 * tokens * width),
         name="rear",
     )(
-        where, q, kv, lse, cosine, sine, gain.reshape(1, width), dn,
+        where, q, kv, lse, cosine, sine, gain.reshape(1, width), gain1.reshape(1, width), dn,
         n2, n_all, og, og_all, og_far, wg, wu, wd, wq, wk, wv, wo,
-        resid, n1p, n1_all, att, att_all, out_part,
+        resid, n1p, n1_all, att, att_all, out_part, x,
     )
 
 
@@ -1287,25 +1375,18 @@
         out_part, dn, n_all, n1_all, att_all, grad_far = middle(
             normed2, grad_low, w_gate, w_up, w_down, n1p, attended, grad_all, ndp, nctx
         )
-        down_z, gate_z, up_z, att_z, front_part, front_got, out_got, d_resid, g_mlp_gain = rear(
-            where, query, kv, lse, cosine, sine, mlp_gain, dn, normed2, n_all, grad_low, grad_all, grad_far,
-            w_gate, w_up, w_down, w_query, w_key, w_value, w_out, resid, n1p, n1_all, attended, att_all,
-            out_part, ndp, nctx,
-        )
-        output = resid + (out_part.astype(F32) + out_got.astype(F32))
-        output = output.astype(BF).reshape(seqs, span, width)
+        down_z, gate_z, up_z, att_z, _, _, _, output, d_input, gains = rear(
+            where, query, kv, lse, cosine, sine, mlp_gain, attn_gain, dn, normed2, n_all, grad_low,
+            grad_all, grad_far, w_gate, w_up, w_down, w_query, w_key, w_value, w_out, resid, n1p, n1_all,
+            attended, att_all, out_part, low, ndp, nctx,
+        )
+        output = output.reshape(seqs, span, width)
+        d_input = d_input.reshape(seqs, span, width)
         s_down = jnp.swapaxes(down_z, 1, 2).reshape(w_down.shape[0], -1).astype(F32)
         s_gate, s_up = gate_z.astype(F32), up_z.astype(F32)
         s_att = jnp.sum(att_z.astype(F32), axis=0)
         s_query, s_key = s_att[:, :nq], s_att[:, nq : nq + kvw]
         s_value, s_out = s_att[:, nq + kvw : nq + 2 * kvw], s_att[:, nq + 2 * kvw :].T
-        d_normed1 = front_part.astype(F32) + front_got.astype(F32)
-        d_rows_norm, g_attn_gain = norm_back(low.astype(F32), attn_gain, d_normed1)
-        d_input = (d_resid + d_rows_norm).reshape(seqs, span, width)
-        gains = jnp.stack([g_attn_gain, g_mlp_gain[0]])
-        gains = jnp.swapaxes(gains.reshape(2, ndp * nctx, -1), 0, 1)
-        gains = lax.all_to_all(gains, ("dp", "ctx"), 0, 0, tiled=True)
-        gains = jnp.sum(gains, axis=0)
         return (
             output,
             d_input,

time: 343 us -> 329 us (0.959)
  other arithmetic: 17.6 us -> 7.68 us
  starting transfers between devices: 5.67 us -> 0 us
    all_to_all x1 -> x0, starting transfers between devices: 5.67 us -> none  [local(): gains = lax.all_to_all(gains, ('dp', 'ctx'), 0, 0, tiled=True)]
    reduce_sum x3 -> x0, other arithmetic: 4.36 us -> none  [the longest x1 2.82 us: norm_back(): d_gain = jnp.sum(grad * unit, axis=0)]
    reshape x2 -> x0, other arithmetic: 3.51 us -> none  [the longest x1 2.07 us: local(): d_input = (d_resid + d_rows_norm).reshape(seqs, span, width)]
  transfers between devices with their start and end apart: 1 -> 0, of which waited for: 0 -> 0; matrix products, arithmetic and copies ran while one was open for 4% -> 0% of each run, Pallas kernels for 0% -> 0%
where the time goes in v2:
time: 329 us; the launch traced here: 326 us
  Pallas kernels  308 us (94%)
  local copies, waits for them, and re-layouts  8.97 us (3%)
  other arithmetic  7.68 us (2%)
    pallas_call x1, Pallas kernels, rear(): pl.pallas_call(functools.partial(rear_kernel, ndp, nctx, qw // kvw, chunk...  194 us
    pallas_call x1, Pallas kernels, middle(): pl.pallas_call(functools.partial(middle_kernel, ndp, nctx), grid=(units /...  59.2 us
    pallas_call x1, Pallas kernels, front(): pl.pallas_call(functools.partial(front_kernel, ndp, nctx, group), in_spec...  54 us

profile of v2, /device:TPU:25, one launch (start us, length us, event | category | flops | bytes accessed | tf_op | source)
XLA Modules:
  0.0 325.7 jit_solution(6185881340513152360)
XLA Ops:
  1.3 0.6 pad_add_fusion.where_ref
  1.9 0.5 fusion
  2.4 1.0 pad_maximum_fusion
  3.4 54.0 %front.1 = (bf16[4,256,512]{2,1,0:T(8,128)(2,1)}, bf16[256,1024]{1,0:T(8,128)(2,1)}, bf16[1024,512]{1,0:T(8,128)(2,1)}, bf16[256,1024]{1,0:T(8,128)(2,1)}, f32[1...) custom-call(s32[2]{0:T(128)} %pad_add_fusion.where_ref, ...), custom_call_target="tpu_custom_call" | custom-call | flops 2684354560 | bytes 10485760 | tf_op jit(solution)/shard_map/front/pallas_call | solution.py:269
  57.4 59.2 %middle.1 = (bf16[256,2048]{1,0:T(8,128)(2,1)}, bf16[256,2048]{1,0:T(8,128)(2,1)}, bf16[4,256,2048]{2,1,0:T(8,128)(2,1)}, bf16[4,256,512]{2,1,0:T(8,128)(2,1)}, ...) custom-call(bf16[256,2048]{1,0:T(8,128)(2,1)} %get-tuple-element.35.n_ref.n_hbm.n_own, ...), custom_call_target="tpu_custom_call" | custom-call | flops 25769803776 | bytes 50331648 | tf_op jit(solution)/shard_map/middle/pallas_call | solution.py:464
  116.7 194.3 %rear.1 = (bf16[4,128,1024]{2,1,0:T(8,128)(2,1)}, bf16[128,4096]{1,0:T(8,128)(2,1)}, bf16[128,4096]{1,0:T(8,128)(2,1)}, bf16[4,128,2560]{2,1,0:T(8,128)(2,1)}, b...) custom-call(s32[2]{0:T(128)} %pad_add_fusion.where_ref, ...), custom_call_target="tpu_custom_call" | custom-call | flops 25769803776 | bytes 8388608 | tf_op jit(solution)/shard_map/rear/pallas_call | solution.py:999
  310.9 1.3 slice_bitcast_fusion.1
  312.2 2.3 convert_reduce_fusion
  314.5 0.0 copy-start.3
  314.5 0.7 fusion.1
  315.2 0.9 slice_bitcast_fusion
  316.1 0.0 copy-start.2
  316.1 1.0 copy.34
  317.1 0.0 copy-done.3
  317.1 1.5 convert_element_type.35
  318.6 0.0 copy-done.2
  318.6 0.0 copy-start.1
  318.6 1.5 convert_element_type.36
  320.2 0.0 copy-done.1
  320.2 0.2 convert_bitcast_fusion
  320.4 0.0 copy-start.4
  320.4 1.8 copy.33
  322.2 0.0 copy-start
  322.2 0.0 copy-done.4
  322.2 1.0 copy.38
  323.2 1.0 copy-done
  324.2 1.3 copy.39
  (2 shorter events, 0.0 us)
Async XLA Ops:
  314.5 2.6 copy-start.3
  316.1 2.5 copy-start.2
  318.6 1.5 copy-start.1
  320.4 1.8 copy-start.4
  322.2 2.0 copy-start

commit v3 on v2

--- a/solution.py
+++ b/solution.py
@@ -499,7 +499,7 @@
     resid_hbm, n1_own, n1_near, att_own, att_near, out_hbm, x_hbm,
     down_z, gate_z, up_z, att_z, front_got, out_got, dr_out, output, input_grad, gains_ref,
     n_all, g_all, acts, wg_buf, wu_buf, wd_buf, give, take, x_give, x_take, x_keep,
-    left1, left2, right1, right2, prod, low, d_att, bias_ref, dkv, land, acc,
+    left1, left2, right1, right2, prod, low, bias_ref, dkv, land, acc,
     gain_grad_ref, gains, gains_x, gains_z,
     in_sem, l_sem, w_sem, back_sem, dn_sem, low_sem, dkv_sem, r_sem, core_sem, x_sem, zz_sem, z_own,
     att_sem, y_sem, save_sem, far_sem, tail_sem, gx_sem, gz_sem,
@@ -638,10 +638,19 @@
         remote(give.at[w % 2], take.at[w % 2], core_sem.at[0, w], core_sem.at[1, w], {"ctx": me ^ 1})
         for w in range(3)
     ]
-    x_copies = [
-        remote(x_give.at[w], x_take.at[w], x_sem.at[0, w], x_sem.at[1, w], {"ctx": me ^ 2})
-        for w in range(3)
-    ]
+
+    def z_rows(k):
+        return pl.ds(pl.multiple_of(k * part, part), part)
+
+    def x_copies(w):
+        some = [z_rows(lax.rem(z + s, ndp)) for s in range(1, ndp)] + [z_rows(z)]
+        return [
+            remote(
+                x_give.at[w, at], x_take.at[w, at], x_sem.at[0, w, s], x_sem.at[1, w, s],
+                {"ctx": me ^ 2},
+            )
+            for s, at in enumerate(some)
+        ]
 
     def hand(w):
         give[w % 2, 0] = product(w, 1 - xpos, 1 - core).astype(BF)
@@ -653,7 +662,8 @@
         core_copies[w].wait()
         x_give[w] = (there + take[w % 2, 0].astype(F32)).astype(BF)
         if w < 2:
-            x_copies[w].start()
+            for copy in x_copies(w):
+                copy.start()
         x_keep[w] = (product(w, xpos, core) + take[w % 2, 1].astype(F32)).astype(BF)
 
     hand(0)
@@ -662,9 +672,6 @@
     keep(1)
     hand(2)
     keep(2)
-
-    def z_rows(k):
-        return pl.ds(pl.multiple_of(k * part, part), part)
 
     z_units = pl.ds(pl.multiple_of(start, units), units)
 
@@ -687,11 +694,12 @@
         return pltpu.make_async_copy(x_keep.at[w, z_rows(z)], landing(w), z_own.at[w])
 
     def serve(w):
-        x_copies[w].wait()
-        x_keep[w] = (x_keep[w].astype(F32) + x_take[w].astype(F32)).astype(BF)
-        for copy in z_copies(w):
-            copy.start()
-        z_own_copy(w).start()
+        onward = z_copies(w) + [z_own_copy(w)]
+        for s, copy in enumerate(x_copies(w)):
+            at = z_rows(lax.rem(z + 1 + s, ndp))
+            copy.wait()
+            x_keep[w, at] = (x_keep[w, at].astype(F32) + x_take[w, at].astype(F32)).astype(BF)
+            onward[s].start()
 
     wo, wq = n_all, acts.at[pl.ds(0, width)]
     wk, wv = wg_buf.at[0], wu_buf.at[0]
@@ -760,6 +768,7 @@
         copy.start()
     left2[mine, :] = give[0, 0, low_rows(me), low_cols(me)]
     loads[0].wait()
+    d_att = give.at[1, 0, pl.ds(0, span)]
     d_att[...] = nt(low[...], wo[...]).astype(BF)
     wide = 128 * group
     heads = wide // HD
@@ -833,7 +842,8 @@
     )
     r_x.start()
     r_core.start()
-    x_copies[2].start()
+    for copy in x_copies(2):
+        copy.start()
     loads[2].wait()
     loads[3].wait()
     low[...] = (
@@ -1030,7 +1040,6 @@
             pltpu.VMEM((length, qw), BF),
             pltpu.VMEM((mine, qkvw + qw), BF),
             pltpu.VMEM((span, width), BF),
-            pltpu.VMEM((span, qw), BF),
             pltpu.VMEM((length, span), F32),
             pltpu.VMEM((kvw // 128, length, 256), BF),
             pltpu.VMEM((kvw // 128, nctx, span, 256), BF),
@@ -1048,7 +1057,7 @@
             dma((2, kvw // 128, nctx)),
             dma((2, 3)),
             dma((2, 3)),
-            dma((2, 3)),
+            dma((2, 3, ndp)),
             dma((2, 3, ndp)),
             dma((3,)),
             dma((2, 2, ndp)),

time: 329 us -> 327 us (level)
  no operation moved by 1% of the time
where the time goes in v3:
time: 327 us; the launch traced here: 323 us
  Pallas kernels  305 us (93%)
  local copies, waits for them, and re-layouts  8.97 us (3%)
  other arithmetic  7.68 us (2%)
    pallas_call x1, Pallas kernels, rear(): pl.pallas_call(functools.partial(rear_kernel, ndp, nctx, qw // kvw, chunk...  192 us
    pallas_call x1, Pallas kernels, middle(): pl.pallas_call(functools.partial(middle_kernel, ndp, nctx), grid=(units /...  59.2 us
    pallas_call x1, Pallas kernels, front(): pl.pallas_call(functools.partial(front_kernel, ndp, nctx, group), in_spec...  54 us

profile of v3, /device:TPU:25, one launch (start us, length us, event | category | flops | bytes accessed | tf_op | source)
XLA Modules:
  0.0 323.1 jit_solution(7449754014155316791)
XLA Ops:
  1.3 0.6 pad_add_fusion.where_ref
  1.9 0.5 fusion
  2.4 1.0 pad_maximum_fusion
  3.4 54.0 %front.1 = (bf16[4,256,512]{2,1,0:T(8,128)(2,1)}, bf16[256,1024]{1,0:T(8,128)(2,1)}, bf16[1024,512]{1,0:T(8,128)(2,1)}, bf16[256,1024]{1,0:T(8,128)(2,1)}, f32[1...) custom-call(s32[2]{0:T(128)} %pad_add_fusion.where_ref, ...), custom_call_target="tpu_custom_call" | custom-call | flops 2684354560 | bytes 10485760 | tf_op jit(solution)/shard_map/front/pallas_call | solution.py:269
  57.4 59.2 %middle.1 = (bf16[256,2048]{1,0:T(8,128)(2,1)}, bf16[256,2048]{1,0:T(8,128)(2,1)}, bf16[4,256,2048]{2,1,0:T(8,128)(2,1)}, bf16[4,256,512]{2,1,0:T(8,128)(2,1)}, ...) custom-call(bf16[256,2048]{1,0:T(8,128)(2,1)} %get-tuple-element.35.n_ref.n_hbm.n_own, ...), custom_call_target="tpu_custom_call" | custom-call | flops 25769803776 | bytes 50331648 | tf_op jit(solution)/shard_map/middle/pallas_call | solution.py:464
  116.7 191.6 %rear.1 = (bf16[4,128,1024]{2,1,0:T(8,128)(2,1)}, bf16[128,4096]{1,0:T(8,128)(2,1)}, bf16[128,4096]{1,0:T(8,128)(2,1)}, bf16[4,128,2560]{2,1,0:T(8,128)(2,1)}, b...) custom-call(s32[2]{0:T(128)} %pad_add_fusion.where_ref, ...), custom_call_target="tpu_custom_call" | custom-call | flops 25769803776 | bytes 8388608 | tf_op jit(solution)/shard_map/rear/pallas_call | solution.py:1009
  308.3 1.3 slice_bitcast_fusion.1
  309.6 2.3 convert_reduce_fusion
  311.9 0.0 copy-start.3
  311.9 0.7 fusion.1
  312.6 0.9 slice_bitcast_fusion
  313.5 0.0 copy-start.2
  313.5 1.0 copy.34
  314.5 0.0 copy-done.3
  314.5 1.5 convert_element_type.35
  316.0 0.0 copy-done.2
  316.0 0.0 copy-start.1
  316.0 1.5 convert_element_type.36
  317.5 0.0 copy-done.1
  317.5 0.2 convert_bitcast_fusion
  317.8 0.0 copy-start.4
  317.8 1.8 copy.33
  319.6 0.0 copy-start
  319.6 0.0 copy-done.4
  319.6 1.0 copy.38
  320.6 1.0 copy-done
  321.5 1.3 copy.39
  (2 shorter events, 0.0 us)
Async XLA Ops:
  311.9 2.6 copy-start.3
  313.5 2.5 copy-start.2
  316.0 1.5 copy-start.1
  317.8 1.8 copy-start.4
  319.6 2.0 copy-start
